TPU v7x, 32 devices: a whole 2x2x4 slice. The times are simulated.
32 devices in a mesh: grp: 4 (over y, core), slab: 8 (over z, x).
Axes of the slice: x: 2, y: 2, z: 4, core: 2. Of those that a mesh axis runs over, the one named last changes fastest.
Arguments:
- velocity: float32 [3, 32, 144, 512], P(None, 'slab', None, 'grp'), may hold values from -6 to 6
- w_in: bfloat16 [27, 16, 3], replicated, may hold values from -0.625 to 0.625
- w_mid_a: bfloat16 [27, 16, 16], replicated, may hold values from -0.3125 to 0.3125
- w_mid_b: bfloat16 [27, 16, 16], replicated, may hold values from -0.3125 to 0.3125
- w_out: bfloat16 [27, 6, 16], replicated, may hold values from -0.3125 to 0.3125
Outputs:
- velocity_next: float32 [3, 32, 144, 512], P(None, 'slab', None, 'grp')
- stress: bfloat16 [6, 16, 72, 256], P(None, 'slab', 'grp')
- grad_in: float32 [27, 16, 3], replicated
- grad_mid_a: float32 [27, 16, 16], replicated
- grad_mid_b: float32 [27, 16, 16], replicated
- grad_out: float32 [27, 6, 16], replicated
All inputs are finite; a program needn't handle non-finite values.
Results may differ from a plain program's by a relative error of at most 0.0071.
Values may be sent and summed in bfloat16 or wider, within the bound.
No kernel may reach another device: no remote copies, remote signals or barrier semaphores. Data moves between devices by JAX's collectives and lax.ppermute only.
A program may use at most 448 MiB of HBM per device.

v0:
```python
import jax
import jax.numpy as jnp
from jax import lax
from jax.sharding import PartitionSpec as P

step_size = 0.1
viscosity = 0.5
closure_weight = 4.0
pair_table = ((0, 3, 4), (3, 1, 5), (4, 5, 2))
stress_pairs = ((0, 0), (1, 1), (2, 2), (0, 1), (0, 2), (1, 2))


def with_halo(cells, sides, width):
    for axis, dim in sides:
        count = lax.axis_size(axis)
        head = lax.slice_in_dim(cells, 0, width, axis=dim)
        tail = lax.slice_in_dim(cells, cells.shape[dim] - width, cells.shape[dim], axis=dim)
        cells = jnp.concatenate(
            [
                lax.ppermute(tail, axis, [(i, (i + 1) % count) for i in range(count)]),
                cells,
                lax.ppermute(head, axis, [((i + 1) % count, i) for i in range(count)]),
            ],
            axis=dim,
        )
    return cells


def gradient_along(padded, along):
    length = padded.shape[along] - 4

    def window_at(offset):
        return lax.slice_in_dim(padded, offset, offset + length, axis=along)

    return (window_at(0) - 8.0 * window_at(1) + 8.0 * window_at(3) - window_at(4)) / 12.0


def laplace_along(padded, along):
    length = padded.shape[along] - 4

    def window_at(offset):
        return lax.slice_in_dim(padded, offset, offset + length, axis=along)

    return (
        -window_at(0)
        + 16.0 * window_at(1)
        - 30.0 * window_at(2)
        + 16.0 * window_at(3)
        - window_at(4)
    ) / 12.0


def wall_ghosts(interior):
    return jnp.pad(interior, ((0, 0), (0, 0), (2, 2), (0, 0)))


def stress_force(extended):
    inner_x = extended[:, :, :, 2:-2]
    inner_z = extended[:, 2:-2]
    walled = wall_ghosts(extended[:, 2:-2, :, 2:-2])
    components = []
    for along_x, along_y, along_z in pair_table:
        summed = gradient_along(inner_x[along_x : along_x + 1], 1)
        summed = summed + gradient_along(walled[along_y : along_y + 1], 2)
        summed = summed + gradient_along(inner_z[along_z : along_z + 1], 3)
        components.append(-closure_weight * summed)
    return jnp.concatenate(components, axis=0)


def tendency(extended, forcing):
    inner_x = extended[:, :, :, 2:-2]
    inner_z = extended[:, 2:-2]
    interior = extended[:, 2:-2, :, 2:-2]
    walled = wall_ghosts(interior)
    advect = interior[0:1] * gradient_along(inner_x, 1)
    advect = advect + interior[1:2] * gradient_along(walled, 2)
    advect = advect + interior[2:3] * gradient_along(inner_z, 3)
    diffuse = laplace_along(inner_x, 1) + laplace_along(walled, 2) + laplace_along(inner_z, 3)
    return -advect + viscosity * diffuse + forcing


def block_mean(field):
    comps, cells_x, cells_y, cells_z = field.shape
    return field.reshape(comps, cells_x // 2, 2, cells_y // 2, 2, cells_z // 2, 2).mean(
        axis=(2, 4, 6)
    )


def filter_fields(velocity):
    block_means = block_mean(velocity)
    products = jnp.stack(
        [velocity[left_comp] * velocity[right_comp] for left_comp, right_comp in stress_pairs]
    )
    resolved = jnp.stack(
        [block_means[left_comp] * block_means[right_comp] for left_comp, right_comp in stress_pairs]
    )
    return jnp.concatenate([block_means, block_mean(products) - resolved], axis=0).astype(
        jnp.bfloat16
    )


def prolong(coarse):
    return jnp.repeat(jnp.repeat(jnp.repeat(coarse, 2, axis=1), 2, axis=2), 2, axis=3)


def extend_depth(activation):
    rimmed = with_halo(activation, (("grp", 2), ("slab", 1)), 1)
    place = lax.axis_index("grp")
    count = lax.axis_size("grp")
    rows = jnp.arange(rimmed.shape[2])
    keep = ((rows > 0) | (place > 0)) & ((rows < rimmed.shape[2] - 1) | (place < count - 1))
    return rimmed * keep[None, None, :, None].astype(rimmed.dtype)


def shifted_stack(padded):
    in_ch = padded.shape[0]
    outer_rows = padded.shape[1] - 2
    middle_rows = padded.shape[2] - 2
    stacked = jnp.stack(
        [
            padded[:, shift_a : shift_a + outer_rows, shift_b : shift_b + middle_rows, :]
            for shift_a in range(3)
            for shift_b in range(3)
        ]
    )
    return stacked.reshape(9 * in_ch, outer_rows * middle_rows * padded.shape[3])


def convolve(padded, weight):
    out_ch, in_ch = (weight.shape[1], weight.shape[2])
    outer_rows = padded.shape[1] - 2
    middle_rows = padded.shape[2] - 2
    inner_rows = padded.shape[3]
    columns = shifted_stack(padded)
    kernel = weight.reshape(3, 3, 3, out_ch, in_ch)
    summed = jnp.zeros((out_ch, outer_rows, middle_rows, inner_rows), jnp.float32)
    for shift_z in range(3):
        flat_kernel = jnp.transpose(kernel[:, :, shift_z], (2, 0, 1, 3)).reshape(out_ch, 9 * in_ch)
        partial_value = jnp.dot(flat_kernel, columns, preferred_element_type=jnp.float32)
        partial_value = partial_value.reshape(out_ch, outer_rows, middle_rows, inner_rows)
        summed = summed + jnp.roll(partial_value, 1 - shift_z, axis=3)
    return summed


def weight_gradient(cotangent, padded):
    out_ch = cotangent.shape[0]
    in_ch = padded.shape[0]
    columns = shifted_stack(padded)
    partials = []
    for shift_z in range(3):
        moved = jnp.roll(cotangent, shift_z - 1, axis=3).reshape(out_ch, columns.shape[1])
        partial_value = lax.dot_general(
            moved, columns, (((1,), (1,)), ((), ())), preferred_element_type=jnp.float32
        )
        partials.append(jnp.transpose(partial_value.reshape(out_ch, 3, 3, in_ch), (1, 2, 0, 3)))
    return jnp.stack(partials, axis=2).reshape(27, out_ch, in_ch)


def flip_weight(weight):
    out_ch, in_ch = (weight.shape[1], weight.shape[2])
    kernel = weight.reshape(3, 3, 3, out_ch, in_ch)[::-1, ::-1, ::-1]
    return jnp.transpose(kernel, (0, 1, 2, 4, 3)).reshape(27, in_ch, out_ch)


def advance(velocity, stress_x):
    rimmed = with_halo(stress_x, (("grp", 3), ("slab", 1)), 2)
    forcing = stress_force(prolong(rimmed.astype(jnp.float32)))
    extended = with_halo(velocity.astype(jnp.bfloat16), (("grp", 3), ("slab", 1)), 4).astype(
        velocity.dtype
    )
    first_section = extended[:, 2:-2, :, 2:-2] + step_size * tendency(extended, forcing)
    second = tendency(first_section, forcing[:, 2:-2, :, 2:-2])
    return 0.5 * (velocity + first_section[:, 2:-2, :, 2:-2] + step_size * second)


def local(velocity, w_in, w_mid_a, w_mid_b, w_out):
    group_count = lax.axis_size("grp")
    slab_count = lax.axis_size("slab")
    fields = filter_fields(velocity)
    relaid = lax.all_to_all(fields, "grp", split_axis=2, concat_axis=3, tiled=True)
    weights = (w_in, w_mid_a, w_mid_b, w_out)
    activation = relaid[:3]
    target = relaid[3:]
    padded_list = []
    response = None
    for layer_index in range(4):
        padded = extend_depth(activation)
        padded_list.append(padded)
        response = convolve(padded, weights[layer_index])
        if layer_index < 3:
            activation = jnp.tanh(response).astype(jnp.bfloat16)
    stress = response.astype(jnp.bfloat16)
    stress_x = lax.all_to_all(stress, "grp", split_axis=3, concat_axis=2, tiled=True)
    velocity_next = advance(velocity, stress_x)
    length = (
        6 * response.shape[1] * response.shape[2] * response.shape[3] * group_count * slab_count
    )
    cotangent = (2.0 / length * (response - target.astype(jnp.float32))).astype(jnp.bfloat16)
    gradients = [None, None, None, None]
    for layer_index in (3, 2, 1, 0):
        padded = padded_list[layer_index]
        local_grad = weight_gradient(cotangent, padded)
        gradients[layer_index] = local_grad
        if layer_index > 0:
            spread = convolve(extend_depth(cotangent), flip_weight(weights[layer_index]))
            below_act = padded[:, 1:-1, 1:-1, :].astype(jnp.float32)
            cotangent = (spread * (1.0 - below_act * below_act)).astype(jnp.bfloat16)
    summed = lax.psum((gradients[0], gradients[1], gradients[2], gradients[3]), ("grp", "slab"))
    gradients = list(summed)
    return (velocity_next, stress, gradients[0], gradients[1], gradients[2], gradients[3])


def solution(mesh):
    in_specs = (P(None, "slab", None, "grp"), P(), P(), P(), P())
    out_specs = (P(None, "slab", None, "grp"), P(None, "slab", "grp", None), P(), P(), P(), P())
    return jax.shard_map(local, mesh=mesh, in_specs=in_specs, out_specs=out_specs, check_vma=False)
```

profile of v0, /device:TPU:0, one launch (start us, length us, event | category | flops | bytes accessed | tf_op | source)
XLA Modules:
  0.0 973.2 jit_solution(2492821659852501180)
XLA Ops:
  7.2 58.8 %reshape.311 = f32[3,2,2,72,2,64,2]{6,5,4,3,2,1,0:T(8,128)} reshape(f32[3,4,144,128]{3,2,1,0:T(8,128)} %param.5) | data formatting | bytes 1769472 | tf_op jit(solution)/shard_map/reshape | solution.py:84
  66.1 17.7 %reduce_sum.18 = f32[3,2,72,64]{3,2,1,0:T(8,128)S(1)} reduce(f32[3,2,2,72,2,64,2]{6,5,4,3,2,1,0:T(8,128)} %reshape.311, f32[]{:T(128)} %constant.54.clone.1), dimensions={2,4,6}, to_apply=%region_0.0 | reduce | flops 193536 | bytes 995332 | tf_op jit(solution)/shard_map/reduce_sum | solution.py:84
  84.0 20.2 %stack.328 = f32[1,2,2,72,2,64,2]{6,5,4,3,2,1,0:T(8,128)} reshape(f32[1,4,144,128]{3,2,1,0:T(8,128)S(1)} %get-tuple-element.56) | data formatting | bytes 589824 | tf_op jit(solution)/shard_map/stack | solution.py:91
  104.2 13.0 %constant_dynamic-update-slice_fusion.5 = f32[6,2,2,72,2,64,2]{6,5,4,3,2,1,0:T(8,128)} fusion(f32[1,2,2,72,2,64,2]{6,5,4,3,2,1,0:T(8,128)} %stack.328), kind=kLoop, calls=%fused_computation.291 | loop fusion | bytes 19169280
  117.3 20.2 %stack.329 = f32[1,2,2,72,2,64,2]{6,5,4,3,2,1,0:T(8,128)} reshape(f32[1,4,144,128]{3,2,1,0:T(8,128)S(1)} %get-tuple-element.57) | data formatting | bytes 589824 | tf_op jit(solution)/shard_map/stack | solution.py:91
  137.5 20.2 %stack.330 = f32[1,2,2,72,2,64,2]{6,5,4,3,2,1,0:T(8,128)} reshape(f32[1,4,144,128]{3,2,1,0:T(8,128)S(1)} %get-tuple-element.58) | data formatting | bytes 589824 | tf_op jit(solution)/shard_map/stack | solution.py:91
  157.7 20.2 %stack.331 = f32[1,2,2,72,2,64,2]{6,5,4,3,2,1,0:T(8,128)} reshape(f32[1,4,144,128]{3,2,1,0:T(8,128)S(1)} %get-tuple-element.54) | data formatting | bytes 589824 | tf_op jit(solution)/shard_map/stack | solution.py:91
  177.8 20.2 %stack.332 = f32[1,2,2,72,2,64,2]{6,5,4,3,2,1,0:T(8,128)} reshape(f32[1,4,144,128]{3,2,1,0:T(8,128)S(1)} %get-tuple-element.55) | data formatting | bytes 589824 | tf_op jit(solution)/shard_map/stack | solution.py:91
  198.1 20.2 %stack.333 = f32[1,2,2,72,2,64,2]{6,5,4,3,2,1,0:T(8,128)} reshape(f32[1,4,144,128]{3,2,1,0:T(8,128)S(1)} %get-tuple-element.53) | data formatting | bytes 589824 | tf_op jit(solution)/shard_map/stack | solution.py:91
  218.2 13.1 %constant_dynamic-update-slice_fusion.4 = f32[6,2,2,72,2,64,2]{6,5,4,3,2,1,0:T(8,128)} fusion(f32[6,2,2,72,2,64,2]{6,5,4,3,2,1,0:T(8,128)} %constant_dynamic-update-slice_fusion.5, f32[1,2,2,72,2,64,2]{6,5,4,3,2,1,0:T(8,128)} %stack.329), kind=kLoop, calls=%fused_computation.290 | loop fusion | bytes 37748736
  231.3 15.2 %constant_dynamic-update-slice_fusion.3 = f32[6,2,2,72,2,64,2]{6,5,4,3,2,1,0:T(8,128)} fusion(f32[6,2,2,72,2,64,2]{6,5,4,3,2,1,0:T(8,128)} %constant_dynamic-update-slice_fusion.4, f32[1,2,2,72,2,64,2]{6,5,4,3,2,1,0:T(8,128)} %stack.330), kind=kLoop, calls=%fused_computation.289 | loop fusion | bytes 37748736
  246.5 15.5 %constant_dynamic-update-slice_fusion.2 = f32[6,2,2,72,2,64,2]{6,5,4,3,2,1,0:T(8,128)} fusion(f32[6,2,2,72,2,64,2]{6,5,4,3,2,1,0:T(8,128)} %constant_dynamic-update-slice_fusion.3, f32[1,2,2,72,2,64,2]{6,5,4,3,2,1,0:T(8,128)} %stack.331), kind=kLoop, calls=%fused_computation.288 | loop fusion | bytes 37748736
  262.0 10.0 %constant_dynamic-update-slice_fusion.1 = f32[6,2,2,72,2,64,2]{6,5,4,3,2,1,0:T(8,128)} fusion(f32[6,2,2,72,2,64,2]{6,5,4,3,2,1,0:T(8,128)} %constant_dynamic-update-slice_fusion.2, f32[1,2,2,72,2,64,2]{6,5,4,3,2,1,0:T(8,128)S(1)} %bitcast.600), kind=kLoop, calls=%fused_computation.287 | loop fusion | bytes 19169280
  273.8 7.9 constant_dynamic-update-slice_fusion
  281.7 34.5 %reduce_sum.19 = f32[6,2,72,64]{3,2,1,0:T(8,128)S(1)} reduce(f32[6,2,2,72,2,64,2]{6,5,4,3,2,1,0:T(8,128)} %constant_dynamic-update-slice_fusion, f32[]{:T(128)} %constant.54.clone.1), dimensions={2,4,6}, to_apply=%region_1.0 | reduce | flops 387072 | bytes 1990660 | tf_op jit(solution)/shard_map/reduce_sum | solution.py:84
  317.6 4.4 all-to-all-start
  335.8 3.1 collective-permute-start.7
  362.2 3.4 collective-permute-start.11
  366.3 4.8 collective-permute-done.10
  381.5 4.1 reshape.320
  407.4 4.4 collective-permute-start.3
  412.2 4.7 collective-permute-start.15
  420.2 5.5 dot_general.195
  425.7 25.1 %collective-permute-done.14 = bf16[16,1,20,256]{3,2,1,0:T(8,128)(2,1)S(1)} collective-permute-done((bf16[16,1,20,256]{3,2,1,0:T(8,128)(2,1)S(1)}, bf16[16,1,20,256]{3,2,1,0:T(8,128)(2,1)S(1)}, u32[]{:S(2)}, u32[]{:S(2)}) %collective-permute-start.14) | collective-permute-done | bytes 163872 | tf_op jit(solution)/shard_map/ppermute | solution.py:20
  461.6 4.1 reshape.328
  487.0 4.9 collective-permute-start.19
  495.9 5.5 dot_general.199
  509.5 4.1 reshape.336
  530.7 4.1 dot_general.203
  546.6 4.0 convolution_bitcast_fusion.29
  550.6 2.9 convolution_bitcast_fusion.27
  555.3 3.0 convolution_bitcast_fusion.28
  561.1 5.1 collective-permute-start.27
  568.8 3.3 all-to-all-start.1
  591.7 4.6 convolution_bitcast_fusion.23
  596.4 3.6 convolution_bitcast_fusion.22
  600.4 3.0 convolution_bitcast_fusion.21
  612.2 3.5 collective-permute-done.20
  617.6 4.7 collective-permute-start.23
  623.1 4.7 collective-permute-start.31
  627.8 4.2 collective-permute-done.22
  632.0 2.9 collective-permute-done.23
  635.4 4.1 broadcast_in_dim.7
  639.5 6.7 copy.258
  646.2 10.1 %broadcast_in_dim.8 = f32[6,12,144,68,2]{2,4,3,1,0:T(2,128)} broadcast(f32[6,12,144,68]{2,3,1,0:T(8,128)} %copy.258), dimensions={0,1,2,3} | broadcast | bytes 8460288 | tf_op jit(solution)/shard_map/broadcast_in_dim | solution.py:103
  656.3 12.7 %reshape.346 = f32[6,12,144,136]{2,3,1,0:T(8,128)} reshape(f32[6,12,144,68,2]{2,4,3,1,0:T(2,128)} %broadcast_in_dim.8) | data formatting | bytes 11280384 | tf_op jit(solution)/shard_map/reshape | solution.py:103
  669.1 3.6 slice.1249
  677.1 3.9 fusion.13
  681.0 14.0 %fusion.2 = (f32[3,8,144,132]{2,3,1,0:T(8,128)S(1)}, f32[3,8,144,132]{2,3,1,0:T(8,128)}) fusion(f32[3,8,144,132]{2,3,1,0:T(8,128)} %slice.1147, f32[3,12,144,136]{2,3,1,0:T(8,128)S(1)} %bitcast.598, f32[8,144,132]{1,2,0:T(8,128)} %get-tuple-element.46, f32[8,144,132]{1,2,0:T(8,128)} %get-tuple-element.47, f32[8,144,132]{1,2,0:T(8,128)} %get-tuple-element.45, ...), kind=kLoop, calls=%fused_computation.25 | loop fusion | flops 23721984 | bytes 23721984 | tf_op jit(solution)/shard_map/add | solution.py:171
  706.8 5.7 reshape.354
  712.6 3.1 convolution_bitcast_fusion.3
  721.8 3.1 convolution_bitcast_fusion.5
  728.8 3.1 convolution_bitcast_fusion.4
  745.5 5.6 convolution_bitcast_fusion.26
  751.2 4.6 convolution_bitcast_fusion.25
  761.8 4.7 collective-permute-start.35
  766.5 4.8 convolution_bitcast_fusion.24
  782.6 5.7 reshape.361
  788.3 3.1 convolution_bitcast_fusion
  797.5 3.1 convolution_bitcast_fusion.2
  804.6 3.1 convolution_bitcast_fusion.1
  830.1 8.5 fusion.7
  838.6 2.8 copy.279
  841.4 117.8 %all-reduce.6.cloned.1.call-done = (f32[27,16,3]{1,0,2:T(8,128)}, f32[27,16,16]{2,1,0:T(8,128)}, f32[27,16,16]{2,1,0:T(8,128)}, f32[27,6,16]{2,1,0:T(8,128)}) async-done(((f32[27,16,3]{1,0,2:T(8,128)}, f32[27,16,16]{2,1,0:T(8,128)}, f32[27,16,16]{2,1,0:T(8,128)}, f32[27,6,16]{2,1,0:T(8,128)}), (f32[27,16,3]{1,0,2:T(8,128)}, f32[27,16,16]{2,1,0:T(8,128)}, f32[27,16,16]{2,1,0:T(8,128)}, ...) | async-done | bytes 70864 | tf_op jit(solution)/shard_map/psum | solution.py:208
  (512 shorter events, 284.5 us)
Async XLA Ops:
  7.2 58.8 %copy-start.13 = (f32[3,4,144,128]{3,2,1,0:T(8,128)S(1)}, f32[3,4,144,128]{3,2,1,0:T(8,128)}, u32[]{:S(2)}) copy-start(f32[3,4,144,128]{3,2,1,0:T(8,128)} %param.5) | copy-start | bytes 2654212
  231.3 30.7 %slice-start.2 = ((s8[18874368]{0:T(1024)(128)(4,1)}), s8[4194304]{0:T(1024)(128)(4,1)S(1)}, s32[]{:S(2)}) async-start(s8[18874368]{0:T(1024)(128)(4,1)} %bitcast.599), calls=%async_computation.5 | async-start | bytes 8388608
  231.3 30.7 %slice-start.3 = ((s8[18874368]{0:T(1024)(128)(4,1)}), s8[4194304]{0:T(1024)(128)(4,1)S(1)}, s32[]{:S(2)}) async-start(s8[18874368]{0:T(1024)(128)(4,1)} %bitcast.599), calls=%async_computation.6 | async-start | bytes 8388608
  231.3 30.7 %slice-start.4 = ((s8[18874368]{0:T(1024)(128)(4,1)}), s8[4194304]{0:T(1024)(128)(4,1)S(1)}, s32[]{:S(2)}) async-start(s8[18874368]{0:T(1024)(128)(4,1)} %bitcast.599), calls=%async_computation.7 | async-start | bytes 8388608
  246.5 15.5 %slice-start.5 = ((s8[18874368]{0:T(1024)(128)(4,1)}), s8[4194304]{0:T(1024)(128)(4,1)S(1)}, s32[]{:S(2)}) async-start(s8[18874368]{0:T(1024)(128)(4,1)} %bitcast.599), calls=%async_computation.8 | async-start | bytes 8388608
  246.5 15.5 %slice-start.6 = ((s8[18874368]{0:T(1024)(128)(4,1)}), s8[2097152]{0:T(1024)(128)(4,1)S(1)}, s32[]{:S(2)}) async-start(s8[18874368]{0:T(1024)(128)(4,1)} %bitcast.599), calls=%async_computation.9 | async-start | bytes 4194304
  246.5 25.6 %slice-start.7 = ((s8[18874368]{0:T(1024)(128)(4,1)}), s8[4194304]{0:T(1024)(128)(4,1)S(1)}, s32[]{:S(2)}) async-start(s8[18874368]{0:T(1024)(128)(4,1)} %bitcast.601), calls=%async_computation.10 | async-start | bytes 8388608
  246.5 25.6 %slice-start.8 = ((s8[18874368]{0:T(1024)(128)(4,1)}), s8[4194304]{0:T(1024)(128)(4,1)S(1)}, s32[]{:S(2)}) async-start(s8[18874368]{0:T(1024)(128)(4,1)} %bitcast.601), calls=%async_computation.11 | async-start | bytes 8388608
  246.5 25.6 %slice-start.9 = ((s8[18874368]{0:T(1024)(128)(4,1)}), s8[4194304]{0:T(1024)(128)(4,1)S(1)}, s32[]{:S(2)}) async-start(s8[18874368]{0:T(1024)(128)(4,1)} %bitcast.601), calls=%async_computation.12 | async-start | bytes 8388608
  262.0 11.2 %slice-start.10 = ((s8[18874368]{0:T(1024)(128)(4,1)}), s8[4194304]{0:T(1024)(128)(4,1)S(1)}, s32[]{:S(2)}) async-start(s8[18874368]{0:T(1024)(128)(4,1)} %bitcast.601), calls=%async_computation.13 | async-start | bytes 8388608
  262.0 11.8 %slice-start.11 = ((s8[18874368]{0:T(1024)(128)(4,1)}), s8[2097152]{0:T(1024)(128)(4,1)S(1)}, s32[]{:S(2)}) async-start(s8[18874368]{0:T(1024)(128)(4,1)} %bitcast.601), calls=%async_computation.14 | async-start | bytes 4194304
  317.6 12.1 %all-to-all-start = ((bf16[4,2,10368]{2,1,0:T(2,128)(2,1)}), bf16[4,2,10368]{2,1,0:T(2,128)(2,1)S(1)}, u32[]{:S(2)}, u32[]{:S(2)}) async-start(bf16[4,2,10368]{2,1,0:T(2,128)(2,1)} %reshape.410), calls=%async_computation | async-start | bytes 331776 | tf_op jit(solution)/shard_map/all_to_all | solution.py:180
  323.4 81.8 %collective-permute-start = (bf16[3,4,144,4]{2,3,1,0:T(4,128)(2,1)}, bf16[3,4,144,4]{2,3,1,0:T(4,128)(2,1)}, u32[]{:S(2)}, u32[]{:S(2)}) collective-permute-start(bf16[3,4,144,4]{2,3,1,0:T(4,128)(2,1)} %get-tuple-element.59), channel_id=1, source_target_pairs={{0,8},{8,16},{16,24},{24,0},{1,9},{9,17},{17,25},{25,1},{2,10},{10... | collective-permute-start | bytes 41480 | tf_op jit(solution)/shard_map/ppermute | solution.py:20
  323.9 81.3 %collective-permute-start.1 = (bf16[3,4,144,4]{2,3,1,0:T(4,128)(2,1)}, bf16[3,4,144,4]{2,3,1,0:T(4,128)(2,1)}, u32[]{:S(2)}, u32[]{:S(2)}) collective-permute-start(bf16[3,4,144,4]{2,3,1,0:T(4,128)(2,1)} %get-tuple-element.60), channel_id=1, source_target_pairs={{8,0},{16,8},{24,16},{0,24},{9,1},{17,9},{25,17},{1,25},{10,2},{18... | collective-permute-start | bytes 41480 | tf_op jit(solution)/shard_map/ppermute | solution.py:22
  330.1 12.0 %copy-start.29 = (bf16[9,2,4,18,64]{4,2,3,1,0:T(4,128)(2,1)}, bf16[9,2,4,18,64]{4,2,3,1,0:T(4,128)(2,1)S(1)}, u32[]{:S(2)}) copy-start(bf16[9,2,4,18,64]{4,2,3,1,0:T(4,128)(2,1)S(1)} %copy.320) | copy-start | bytes 497668
  330.4 3.1 collective-permute-start.4
  330.9 2.6 collective-permute-start.5
  333.6 7.5 collective-permute-start.6
  335.8 5.3 collective-permute-start.7
  352.2 8.3 collective-permute-start.8
  353.3 7.2 collective-permute-start.9
  360.9 10.2 %collective-permute-start.10 = (bf16[16,1,20,256]{3,2,1,0:T(8,128)(2,1)S(1)}, bf16[16,1,20,256]{3,2,1,0:T(8,128)(2,1)S(1)}, u32[]{:S(2)}, u32[]{:S(2)}) collective-permute-start(bf16[16,1,20,256]{3,2,1,0:T(8,128)(2,1)S(1)} %get-tuple-element.89), channel_id=1, source_target_pairs={{0,1},{1,2},{2,3},{3,4},{4,5},{5,6},{6,7},{7,0},{8,9},{9,10},{10,1... | collective-permute-start | bytes 491528 | tf_op jit(solution)/shard_map/ppermute | solution.py:20
  362.2 11.1 %collective-permute-start.11 = (bf16[16,1,20,256]{3,2,1,0:T(8,128)(2,1)S(1)}, bf16[16,1,20,256]{3,2,1,0:T(8,128)(2,1)S(1)}, u32[]{:S(2)}, u32[]{:S(2)}) collective-permute-start(bf16[16,1,20,256]{3,2,1,0:T(8,128)(2,1)S(1)} %get-tuple-element.90), channel_id=1, source_target_pairs={{1,0},{2,1},{3,2},{4,3},{5,4},{6,5},{7,6},{0,7},{9,8},{10,9},{11,1... | collective-permute-start | bytes 491528 | tf_op jit(solution)/shard_map/ppermute | solution.py:22
  400.9 16.0 %copy-start.30 = (bf16[9,2,4,18,64]{4,2,3,1,0:T(4,128)(2,1)S(1)}, bf16[9,2,4,18,64]{4,2,3,1,0:T(4,128)(2,1)}, u32[]{:S(2)}) copy-start(bf16[9,2,4,18,64]{4,2,3,1,0:T(4,128)(2,1)} %copy-done.29) | copy-start | bytes 497668
  403.0 8.8 collective-permute-start.12
  403.1 16.0 %copy-start.16 = (bf16[9,3,2,18,256]{4,3,2,1,0:T(8,128)(2,1)S(1)}, bf16[9,3,2,18,256]{4,3,2,1,0:T(8,128)(2,1)}, u32[]{:S(2)}) copy-start(bf16[9,3,2,18,256]{4,3,2,1,0:T(8,128)(2,1)} %copy-done.15) | copy-start | bytes 1492996
  403.1 8.7 collective-permute-start.13
  407.1 77.7 %collective-permute-start.2 = (bf16[3,4,144,136]{2,3,1,0:T(8,128)(2,1)}, bf16[3,4,144,136]{2,3,1,0:T(8,128)(2,1)}, u32[]{:S(2)}, u32[]{:S(2)}) collective-permute-start(bf16[3,4,144,136]{2,3,1,0:T(8,128)(2,1)} %pad_maximum_fusion.1), channel_id=1, source_target_pairs={{0,1},{1,2},{2,3},{3,4},{4,5},{5,6},{6,7},{7,0},{8,9},{9,10},{10,1... | collective-permute-start | bytes 1410056 | tf_op jit(solution)/shard_map/ppermute | solution.py:20
  407.4 77.4 %collective-permute-start.3 = (bf16[3,4,144,136]{2,3,1,0:T(8,128)(2,1)}, bf16[3,4,144,136]{2,3,1,0:T(8,128)(2,1)}, u32[]{:S(2)}, u32[]{:S(2)}) collective-permute-start(bf16[3,4,144,136]{2,3,1,0:T(8,128)(2,1)} %pad_maximum_fusion.1), channel_id=1, source_target_pairs={{1,0},{2,1},{3,2},{4,3},{5,4},{6,5},{7,6},{0,7},{9,8},{10,9},{11,1... | collective-permute-start | bytes 1410056 | tf_op jit(solution)/shard_map/ppermute | solution.py:22
  412.1 38.7 %collective-permute-start.14 = (bf16[16,1,20,256]{3,2,1,0:T(8,128)(2,1)S(1)}, bf16[16,1,20,256]{3,2,1,0:T(8,128)(2,1)S(1)}, u32[]{:S(2)}, u32[]{:S(2)}) collective-permute-start(bf16[16,1,20,256]{3,2,1,0:T(8,128)(2,1)S(1)} %get-tuple-element.85), channel_id=1, source_target_pairs={{0,1},{1,2},{2,3},{3,4},{4,5},{5,6},{6,7},{7,0},{8,9},{9,10},{10,1... | collective-permute-start | bytes 491528 | tf_op jit(solution)/shard_map/ppermute | solution.py:20
  412.2 41.2 %collective-permute-start.15 = (bf16[16,1,20,256]{3,2,1,0:T(8,128)(2,1)S(1)}, bf16[16,1,20,256]{3,2,1,0:T(8,128)(2,1)S(1)}, u32[]{:S(2)}, u32[]{:S(2)}) collective-permute-start(bf16[16,1,20,256]{3,2,1,0:T(8,128)(2,1)S(1)} %get-tuple-element.86), channel_id=1, source_target_pairs={{1,0},{2,1},{3,2},{4,3},{5,4},{6,5},{7,6},{0,7},{9,8},{10,9},{11,1... | collective-permute-start | bytes 491528 | tf_op jit(solution)/shard_map/ppermute | solution.py:22
  483.0 3.6 collective-permute-start.16
  483.1 3.6 collective-permute-start.17
  487.0 14.4 %collective-permute-start.18 = (bf16[16,1,20,256]{3,2,1,0:T(8,128)(2,1)S(1)}, bf16[16,1,20,256]{3,2,1,0:T(8,128)(2,1)S(1)}, u32[]{:S(2)}, u32[]{:S(2)}) collective-permute-start(bf16[16,1,20,256]{3,2,1,0:T(8,128)(2,1)S(1)} %get-tuple-element.81), channel_id=1, source_target_pairs={{0,1},{1,2},{2,3},{3,4},{4,5},{5,6},{6,7},{7,0},{8,9},{9,10},{10,1... | collective-permute-start | bytes 491528 | tf_op jit(solution)/shard_map/ppermute | solution.py:20
  487.0 14.3 %collective-permute-start.19 = (bf16[16,1,20,256]{3,2,1,0:T(8,128)(2,1)S(1)}, bf16[16,1,20,256]{3,2,1,0:T(8,128)(2,1)S(1)}, u32[]{:S(2)}, u32[]{:S(2)}) collective-permute-start(bf16[16,1,20,256]{3,2,1,0:T(8,128)(2,1)S(1)} %get-tuple-element.82), channel_id=1, source_target_pairs={{1,0},{2,1},{3,2},{4,3},{5,4},{6,5},{7,6},{0,7},{9,8},{10,9},{11,1... | collective-permute-start | bytes 491528 | tf_op jit(solution)/shard_map/ppermute | solution.py:22
  546.6 8.7 copy-start.20
  546.6 8.7 copy-start.31
  546.6 8.7 copy-start.32
  553.5 6.4 collective-permute-start.24
  554.4 5.6 collective-permute-start.25
  558.3 13.9 %copy-start.18 = (bf16[6,2,18,256]{3,2,1,0:T(8,128)(2,1)S(1)}, bf16[6,2,18,256]{3,2,1,0:T(8,128)(2,1)}, u32[]{:S(2)}) copy-start(bf16[6,2,18,256]{3,2,1,0:T(8,128)(2,1)} %copy-done.17) | copy-start | bytes 331780
  561.0 11.1 %collective-permute-start.26 = (bf16[6,1,20,256]{3,2,1,0:T(8,128)(2,1)S(1)}, bf16[6,1,20,256]{3,2,1,0:T(8,128)(2,1)S(1)}, u32[]{:S(2)}, u32[]{:S(2)}) collective-permute-start(bf16[6,1,20,256]{3,2,1,0:T(8,128)(2,1)S(1)} %get-tuple-element.101), channel_id=1, source_target_pairs={{0,1},{1,2},{2,3},{3,4},{4,5},{5,6},{6,7},{7,0},{8,9},{9,10},{10,1... | collective-permute-start | bytes 184328 | tf_op jit(solution)/shard_map/ppermute | solution.py:20
  561.1 11.1 %collective-permute-start.27 = (bf16[6,1,20,256]{3,2,1,0:T(8,128)(2,1)S(1)}, bf16[6,1,20,256]{3,2,1,0:T(8,128)(2,1)S(1)}, u32[]{:S(2)}, u32[]{:S(2)}) collective-permute-start(bf16[6,1,20,256]{3,2,1,0:T(8,128)(2,1)S(1)} %get-tuple-element.102), channel_id=1, source_target_pairs={{1,0},{2,1},{3,2},{4,3},{5,4},{6,5},{7,6},{0,7},{9,8},{10,9},{11,1... | collective-permute-start | bytes 184328 | tf_op jit(solution)/shard_map/ppermute | solution.py:22
  568.8 38.2 %all-to-all-start.1 = ((bf16[4,2,6912]{2,1,0:T(2,128)(2,1)}), bf16[4,2,6912]{2,1,0:T(2,128)(2,1)S(1)}, u32[]{:S(2)}, u32[]{:S(2)}) async-start(bf16[4,2,6912]{2,1,0:T(2,128)(2,1)} %reshape.412), calls=%async_computation.1 | async-start | bytes 221184 | tf_op jit(solution)/shard_map/all_to_all | solution.py:193
  572.1 387.2 %all-reduce.6.cloned.1.call-start = ((), (), s32[]{:S(2)}) async-start(), calls=%async_computation.2 | async-start | bytes 1204224 | tf_op jit(solution)/shard_map/psum | solution.py:208
  582.9 8.9 copy-start.3
  605.1 6.8 collective-permute-start.28
  605.5 6.4 collective-permute-start.29
  610.1 5.6 collective-permute-start.20
  610.5 6.9 collective-permute-start.21
  611.9 23.0 %copy-start.52 = (bf16[16,2,1,256]{3,2,1,0:T(2,128)(2,1)}, bf16[16,2,1,256]{3,2,1,0:T(2,128)(2,1)S(1)}, u32[]{:S(2)}) copy-start(bf16[16,2,1,256]{3,2,1,0:T(2,128)(2,1)S(1)} %collective-permute-done.28) | copy-start | bytes 49156
  611.9 23.0 %copy-start.54 = (bf16[16,2,1,256]{3,2,1,0:T(2,128)(2,1)}, bf16[16,2,1,256]{3,2,1,0:T(2,128)(2,1)S(1)}, u32[]{:S(2)}) copy-start(bf16[16,2,1,256]{3,2,1,0:T(2,128)(2,1)S(1)} %collective-permute-done.29) | copy-start | bytes 49156
  617.5 14.5 %collective-permute-start.22 = (bf16[6,2,72,68]{3,2,1,0:T(8,128)(2,1)S(1)}, bf16[6,2,72,68]{3,2,1,0:T(8,128)(2,1)S(1)}, u32[]{:S(2)}, u32[]{:S(2)}) collective-permute-start(bf16[6,2,72,68]{3,2,1,0:T(8,128)(2,1)S(1)} %pad_maximum_fusion.16), channel_id=1, source_target_pairs={{0,1},{1,2},{2,3},{3,4},{4,5},{5,6},{6,7},{7,0},{8,9},{9,10},{10,1... | collective-permute-start | bytes 352520 | tf_op jit(solution)/shard_map/ppermute | solution.py:20
  617.6 17.3 %collective-permute-start.23 = (bf16[6,2,72,68]{3,2,1,0:T(8,128)(2,1)S(1)}, bf16[6,2,72,68]{3,2,1,0:T(8,128)(2,1)S(1)}, u32[]{:S(2)}, u32[]{:S(2)}) collective-permute-start(bf16[6,2,72,68]{3,2,1,0:T(8,128)(2,1)S(1)} %pad_maximum_fusion.16), channel_id=1, source_target_pairs={{1,0},{2,1},{3,2},{4,3},{5,4},{6,5},{7,6},{0,7},{9,8},{10,9},{11,1... | collective-permute-start | bytes 352520 | tf_op jit(solution)/shard_map/ppermute | solution.py:22
  623.1 74.6 %collective-permute-start.30 = (bf16[16,1,20,256]{3,2,1,0:T(8,128)(2,1)}, bf16[16,1,20,256]{3,2,1,0:T(8,128)(2,1)S(1)}, u32[]{:S(2)}, u32[]{:S(2)}) collective-permute-start(bf16[16,1,20,256]{3,2,1,0:T(8,128)(2,1)} %get-tuple-element.77), channel_id=1, source_target_pairs={{0,1},{1,2},{2,3},{3,4},{4,5},{5,6},{6,7},{7,0},{8,9},{9,10},{10,1... | collective-permute-start | bytes 491528 | tf_op jit(solution)/shard_map/ppermute | solution.py:20
  623.1 74.6 %collective-permute-start.31 = (bf16[16,1,20,256]{3,2,1,0:T(8,128)(2,1)}, bf16[16,1,20,256]{3,2,1,0:T(8,128)(2,1)}, u32[]{:S(2)}, u32[]{:S(2)}) collective-permute-start(bf16[16,1,20,256]{3,2,1,0:T(8,128)(2,1)} %get-tuple-element.78), channel_id=1, source_target_pairs={{1,0},{2,1},{3,2},{4,3},{5,4},{6,5},{7,6},{0,7},{9,8},{10,9},{11,1... | collective-permute-start | bytes 491528 | tf_op jit(solution)/shard_map/ppermute | solution.py:22
  745.5 12.0 %copy-start.26 = (bf16[16,2,18,255]{3,2,1,0:T(8,128)(2,1)S(1)}, bf16[16,2,18,255]{3,2,1,0:T(8,128)(2,1)}, u32[]{:S(2)}) copy-start(bf16[16,2,18,255]{3,2,1,0:T(8,128)(2,1)} %get-tuple-element.66) | copy-start | bytes 881284
  755.8 4.6 collective-permute-start.32
  755.8 4.6 collective-permute-start.33
  758.5 12.9 %copy-start.37 = (f32[3,3,1,16,16]{4,3,1,0,2:T(8,128)S(1)}, f32[3,3,1,16,16]{4,3,1,0,2:T(8,128)}, u32[]{:S(2)}) copy-start(f32[3,3,1,16,16]{4,3,1,0,2:T(8,128)} %convolution_bitcast_fusion.26) | copy-start | bytes 27652
  758.5 12.9 %copy-start.38 = (f32[3,3,1,16,16]{4,3,1,0,2:T(8,128)S(1)}, f32[3,3,1,16,16]{4,3,1,0,2:T(8,128)}, u32[]{:S(2)}) copy-start(f32[3,3,1,16,16]{4,3,1,0,2:T(8,128)} %convolution_bitcast_fusion.25) | copy-start | bytes 27652
  760.4 13.2 %copy-start.10 = (bf16[16,2,18,256]{3,2,1,0:T(8,128)(2,1)S(1)}, bf16[16,2,18,256]{3,2,1,0:T(8,128)(2,1)}, u32[]{:S(2)}) copy-start(bf16[16,2,18,256]{3,2,1,0:T(8,128)(2,1)} %copy-done.9) | copy-start | bytes 884740
  761.7 10.4 %collective-permute-start.34 = (bf16[16,1,20,256]{3,2,1,0:T(8,128)(2,1)S(1)}, bf16[16,1,20,256]{3,2,1,0:T(8,128)(2,1)S(1)}, u32[]{:S(2)}, u32[]{:S(2)}) collective-permute-start(bf16[16,1,20,256]{3,2,1,0:T(8,128)(2,1)S(1)} %get-tuple-element.73), channel_id=1, source_target_pairs={{0,1},{1,2},{2,3},{3,4},{4,5},{5,6},{6,7},{7,0},{8,9},{9,10},{10,1... | collective-permute-start | bytes 491528 | tf_op jit(solution)/shard_map/ppermute | solution.py:20
  761.8 11.8 %collective-permute-start.35 = (bf16[16,1,20,256]{3,2,1,0:T(8,128)(2,1)S(1)}, bf16[16,1,20,256]{3,2,1,0:T(8,128)(2,1)S(1)}, u32[]{:S(2)}, u32[]{:S(2)}) collective-permute-start(bf16[16,1,20,256]{3,2,1,0:T(8,128)(2,1)S(1)} %get-tuple-element.74), channel_id=1, source_target_pairs={{1,0},{2,1},{3,2},{4,3},{5,4},{6,5},{7,6},{0,7},{9,8},{10,9},{11,1... | collective-permute-start | bytes 491528 | tf_op jit(solution)/shard_map/ppermute | solution.py:22
  (54 other events, 267.1 us)
Sparse Core Ops, SparseCore 0:
  830.2 128.9 all-reduce.5
where the time goes:
time: 987 us; the launch traced here: 973 us
  local copies, waits for them, and re-layouts  518 us (52%)
  waiting for transfers between devices  169 us (17%)
  other arithmetic  124 us (13%)
  matrix products  77.3 us (8%)
  starting transfers between devices  68.2 us (7%)
  between operations  15.9 us (2%)
    another operation x7, local copies, waits for them, and re-layouts, filter_fields(): jnp.stack([velocity[left_comp] * velocity[right_comp] for left_comp, righ...  129 us
    unnamed x234, local copies, waits for them, and re-layouts  123 us
    psum x1, waiting for transfers between devices, local(): lax.psum((gradients[0], gradients[1], gradients[2], gradients[3]), ('grp'...  118 us
    reshape x1, local copies, waits for them, and re-layouts, block_mean(): field.reshape(comps, cells_x // 2, 2, cells_y // 2, 2, cells_z // 2, 2)  58.8 us
    ppermute x18, starting transfers between devices, with_halo(): lax.ppermute(head, axis, [((i + 1) % count, i) for i in range(count)])  52.4 us
    reduce_sum x2, other arithmetic, block_mean(): field.reshape(comps, cells_x // 2, 2, cells_y // 2, 2, cells_z // 2, 2)  52.2 us
    dot_general x12, matrix products, weight_gradient(): lax.dot_general(moved, columns, (((1,), (1,)), ((), ())), preferred_eleme...  42.5 us
    ppermute x18, waiting for transfers between devices, with_halo(): lax.ppermute(tail, axis, [(i, (i + 1) % count) for i in range(count)])  40.3 us
  transfers between devices with their start and end apart: 39, of which 13 were waited for; matrix products, arithmetic and copies ran while one was open for 24% of the time, Pallas kernels for 0%

commit v1 on v0

v1 whole, which is shorter than its diff:
```python
import functools

import jax
import jax.numpy as jnp
import numpy as np
from jax import lax
from jax.experimental import pallas as pl
from jax.experimental.pallas import tpu as pltpu
from jax.sharding import PartitionSpec as P

step_size = 0.1
viscosity = 0.5
closure_weight = 4.0
pair_table = ((0, 3, 4), (3, 1, 5), (4, 5, 2))
stress_pairs = ((0, 0), (1, 1), (2, 2), (0, 1), (0, 2), (1, 2))
LAYERS = 4
CH = 16
MARGIN = LAYERS + LAYERS - 1
f32 = jnp.float32
bf16 = jnp.bfloat16
VMEM_LIMIT = 60 * 1024 * 1024


def round_up(a, b):
    return -(-a // b) * b


def log2(n):
    assert n & (n - 1) == 0
    return n.bit_length() - 1


def call(body, out_shape, scratch, cost, n_in):
    many = isinstance(out_shape, (tuple, list))
    spec = pl.BlockSpec(memory_space=pltpu.VMEM)
    return pl.pallas_call(
        body,
        out_shape=out_shape,
        in_specs=[spec] * n_in,
        out_specs=[spec] * len(out_shape) if many else spec,
        scratch_shapes=scratch,
        compiler_params=pltpu.CompilerParams(vmem_limit_bytes=VMEM_LIMIT),
        cost_estimate=pl.CostEstimate(flops=cost, bytes_accessed=cost // 400, transcendentals=0),
    )


def granule_swap(arrays):
    n = len(arrays)
    lanes = arrays[0].shape[1]
    gran = lanes // n
    granule = lax.broadcasted_iota(jnp.int32, arrays[0].shape, 1) >> log2(gran)
    arrays = list(arrays)
    hop = 1
    while hop < n:
        upper = (granule & hop) != 0
        for i in range(n):
            if i & hop:
                continue
            low, high = arrays[i], arrays[i + hop]
            arrays[i] = jnp.where(upper, pltpu.roll(high, hop * gran, 1), low)
            arrays[i + hop] = jnp.where(upper, high, pltpu.roll(low, lanes - hop * gran, 1))
        hop *= 2
    return arrays


def rounded(x):
    return x.astype(bf16).astype(f32)


def filter_kernel(n, v_ref, out_ref, q_ref, f_ref):
    comps, fine_x, fine_y, fine_z = v_ref.shape
    cx, cy, cz = fine_x // 2, fine_y // 2, fine_z // 2
    zl = cz // n
    group = out_ref.shape[1]
    lanes = out_ref.shape[2]

    def chunk(j, carry):
        for xi in range(cx):
            sums = [None] * 9
            for a in range(2):
                for p in range(2):
                    cell = [v_ref[c, 2 * xi + a, pl.ds(16 * j + p, 8, stride=2), :] for c in range(3)]
                    terms = cell + [cell[l] * cell[r] for l, r in stress_pairs]
                    sums = [t if s is None else s + t for s, t in zip(sums, terms)]
            for k in range(9):
                q_ref[pl.ds(pl.multiple_of(k * cy + 8 * j, 8), 8), xi * fine_z : (xi + 1) * fine_z] = sums[k]
        return carry

    lax.fori_loop(0, cy // 8, chunk, 0)
    row = lax.broadcasted_iota(jnp.int32, (cx * fine_z, lanes), 0)
    col = lax.broadcasted_iota(jnp.int32, (cx * fine_z, lanes), 1)
    row_x = row >> log2(fine_z)
    row_z = (row & (fine_z - 1)) >> 1
    col_x = (col & (cx * zl - 1)) >> log2(zl)
    col_z = (col >> log2(cx * zl)) * zl + (col & (zl - 1))
    proj = jnp.where((row_x == col_x) & (row_z == col_z), 0.125, 0.0).astype(f32)
    means = []
    for k in range(9):
        mean = jnp.dot(
            q_ref[k * cy : (k + 1) * cy, :],
            proj,
            precision=lax.Precision.HIGHEST,
            preferred_element_type=f32,
        )
        if k < 3:
            means.append(mean)
        else:
            l, r = stress_pairs[k - 3]
            mean = mean - means[l] * means[r]
        f_ref[k * cy : (k + 1) * cy, :] = mean
    tail = n * group - 9 * cy
    if tail:
        f_ref[9 * cy :, :] = jnp.zeros((tail, lanes), f32)

    def swap(j, carry):
        base = pl.multiple_of(16 * j, 16)
        parts = granule_swap([f_ref[pl.ds(r * group + base, 16), :] for r in range(n)])
        for d in range(n):
            out_ref[d, pl.ds(base, 16), :] = parts[d].astype(bf16)
        return carry

    lax.fori_loop(0, group // 16, swap, 0)


def edge_kernel(v_ref, v16_ref, e_ref):
    comps, fine_x, fine_y, fine_z = v_ref.shape
    row = lax.broadcasted_iota(jnp.int32, (fine_z, 128), 0)
    col = lax.broadcasted_iota(jnp.int32, (fine_z, 128), 1)
    total = jnp.zeros((fine_y, 128), f32)
    for c in range(comps):
        for x in range(fine_x):
            block = v_ref[c, x].astype(bf16)
            base = (c * fine_x + x) * 8
            v16_ref[(c * fine_x + x) * fine_y : (c * fine_x + x + 1) * fine_y, :] = block
            e = col - base
            hit = ((e >= 0) & (e < 4) & (row == e)) | ((e >= 4) & (e < 8) & (row == fine_z - 8 + e))
            total = total + jnp.dot(
                block, jnp.where(hit, 1.0, 0.0).astype(bf16), preferred_element_type=f32
            )
    e_ref[...] = total.astype(bf16)


def closure_kernel(dims, *refs):
    n, hops, groups, devices, cy, cx, zl, length = dims
    nt = 2 * hops + 1
    tiles = refs[:nt]
    wf_ref, wb_ref, idx_ref = refs[nt : nt + 3]
    bsend_ref, ssend_ref, grad_ref = refs[nt + 3 : nt + 6]
    acts = refs[nt + 6 : nt + 10]
    cot_ref, cz_ref, f_ref, fs_ref, g_ref = refs[nt + 10 :]
    group = tiles[0].shape[1]
    lanes = tiles[0].shape[2]
    own = hops * lanes
    zpos = lax.broadcasted_iota(jnp.int32, (CH, lanes), 1) & (zl - 1)
    first_z = zpos == 0
    last_z = zpos == zl - 1

    def tile(value, t):
        t = min(max(t, 0), nt - 1)
        return value[:, t * lanes : (t + 1) * lanes]

    def after(value, t):
        return jnp.where(
            last_z, pltpu.roll(tile(value, t + 1), zl - 1, 1), pltpu.roll(tile(value, t), lanes - 1, 1)
        )

    def before(value, t):
        return jnp.where(
            first_z,
            pltpu.roll(tile(value, t - 1), lanes - (zl - 1), 1),
            pltpu.roll(tile(value, t), 1, 1),
        )

    def put(ref, y, value):
        for t in range(nt):
            v = tile(value, t)
            at = slice(t * lanes, (t + 1) * lanes)
            ref[y + 1, 0:CH, at] = pltpu.roll(v, zl, 1).astype(bf16)
            ref[y + 1, CH : 2 * CH, at] = v.astype(bf16)
            ref[y + 1, 2 * CH : 3 * CH, at] = pltpu.roll(v, lanes - zl, 1).astype(bf16)

    def put_cz(y, value):
        value = rounded(value)
        cz_ref[y, 0:CH, :] = after(value, hops).astype(bf16)
        cz_ref[y, CH : 2 * CH, :] = tile(value, hops).astype(bf16)
        cz_ref[y, 2 * CH : 3 * CH, :] = before(value, hops).astype(bf16)

    def convolve(src, w, y):
        columns = src[pl.ds(y, 3)].reshape(9 * CH, nt * lanes)
        parts = jnp.dot(w, columns, preferred_element_type=f32)
        low, mid, high = parts[0:CH], parts[CH : 2 * CH], parts[2 * CH :]
        return jnp.concatenate(
            [tile(mid, t) + before(low, t) + after(high, t) for t in range(nt)], axis=1
        )

    for ref in (*acts, cot_ref):
        zero = jnp.zeros((3 * CH, nt * lanes), bf16)
        ref[0] = zero
        ref[cy + 1] = zero
    for t in range(nt):
        used = n * group
        if used < CH * cy:
            f_ref[t, used:, :] = jnp.zeros((CH * cy - used, lanes), f32)

        def swap(j, carry, t=t):
            base = pl.multiple_of(16 * j, 16)
            parts = granule_swap([tiles[t][s, pl.ds(base, 16), :].astype(f32) for s in range(n)])
            for r in range(n):
                f_ref[t, pl.ds(r * group + base, 16), :] = parts[r]
            return carry

        lax.fori_loop(0, group // 16, swap, 0)

    def load_fields(y):
        return jnp.concatenate([f_ref[t, pl.ds(y, CH, stride=cy), :] for t in range(nt)], axis=1)

    def start(y, carry):
        put(acts[0], y, load_fields(y))
        return carry

    lax.fori_loop(0, cy, start, 0)

    for k in range(LAYERS - 1):
        w = wf_ref[k]

        def forward(y, carry, k=k, w=w):
            put(acts[k + 1], y, jnp.tanh(convolve(acts[k], w, y)))
            return carry

        lax.fori_loop(0, cy, forward, 0)

    w_last = wf_ref[LAYERS - 1]
    channel = lax.broadcasted_iota(jnp.int32, (CH, nt * lanes), 0)
    stressed = (channel >= 3) & (channel < 9)

    def predict(y, carry):
        predicted = convolve(acts[LAYERS - 1], w_last, y)
        target = load_fields(y)
        cot = jnp.where(stressed, 2.0 / length * (predicted - target), 0.0)
        put(cot_ref, y, cot)
        put_cz(y, cot)
        stress = rounded(predicted)
        for t in range(nt):
            f_ref[t, pl.ds(y, CH, stride=cy), :] = tile(stress, t)
        return carry

    lax.fori_loop(0, cy, predict, 0)

    def weight_gradient(src, k):
        def pair(j, acc):
            y = 2 * j
            left = jnp.concatenate([cz_ref[y], cz_ref[y + 1]], axis=1)
            right = jnp.concatenate(
                [
                    src[pl.ds(y, 3), :, own : own + lanes].reshape(9 * CH, lanes),
                    src[pl.ds(y + 1, 3), :, own : own + lanes].reshape(9 * CH, lanes),
                ],
                axis=1,
            )
            return acc + lax.dot_general(
                left, right, (((1,), (1,)), ((), ())), preferred_element_type=f32
            )

        g_ref[k] = lax.fori_loop(0, cy // 2, pair, jnp.zeros((3 * CH, 9 * CH), f32))

    weight_gradient(acts[LAYERS - 1], LAYERS - 1)
    source = cot_ref
    for k in range(LAYERS - 1, 0, -1):
        w = wb_ref[k]
        here = acts[k]

        def backward(y, carry, w=w, here=here, source=source, k=k):
            spread = convolve(source, w, y)
            below = here[y + 1, CH : 2 * CH, :].astype(f32)
            cot = spread * (1.0 - below * below)
            if k > 1:
                put(here, y, cot)
            put_cz(y, cot)
            return carry

        lax.fori_loop(0, cy, backward, 0)
        weight_gradient(acts[k - 1], k - 1)
        source = here

    rows = LAYERS * 3 * CH
    main = 8 * CH
    rest = jnp.zeros((rows // 8, main), f32)
    for k in range(LAYERS):
        grad_ref[k * 3 * CH : (k + 1) * 3 * CH, :] = g_ref[k, :, 0:main]
        for half in range(2):
            j = 2 * k + half
            piece = g_ref[k, half * 24 : half * 24 + 24, main:]
            piece = jnp.concatenate([piece, jnp.zeros((24, main - CH), f32)], axis=1)
            rest = rest + (pltpu.roll(piece, j * CH, 1) if j else piece)
    grad_ref[rows : rows + rows // 8, :] = rest
    if grad_ref.shape[0] > rows + rows // 8:
        grad_ref[rows + rows // 8 :, :] = jnp.zeros(
            (grad_ref.shape[0] - rows - rows // 8, main), f32
        )

    left = jnp.concatenate(
        [
            f_ref[t, (3 + 3 * half) * cy : (6 + 3 * half) * cy, :].astype(bf16)
            for half in range(2)
            for t in range(nt)
        ],
        axis=1,
    )
    row = lax.broadcasted_iota(jnp.int32, (2 * nt * lanes, 256), 0)
    for d in range(n // 2):
        pick = jnp.where(row == idx_ref[d], 1.0, 0.0).astype(bf16)
        moved = jnp.dot(left, pick, preferred_element_type=f32).astype(bf16)
        bsend_ref[2 * d] = moved[:, 0:128]
        bsend_ref[2 * d + 1] = moved[:, 128:256]

    wide = cy // groups
    srows = ssend_ref.shape[1]
    fs_ref[...] = jnp.zeros(fs_ref.shape, f32)
    for g in range(groups):
        for c in range(6):
            at = (3 + c) * cy + g * wide
            fs_ref[c * wide : (c + 1) * wide, :] = f_ref[hops, at : at + wide, :]
        for j in range(srows // 16):
            parts = granule_swap(
                [fs_ref[r * srows + 16 * j : r * srows + 16 * j + 16, :] for r in range(n)]
            )
            for d in range(n):
                ssend_ref[g * n + d, 16 * j : 16 * j + 16, :] = parts[d].astype(bf16)


def stress_kernel(n, groups, zl, recv_ref, out_ref, fs_ref):
    comps, cx, wide, depth = out_ref.shape
    srows = recv_ref.shape[1]
    lanes = recv_ref.shape[2]
    cz = n * zl
    for g in range(groups):
        for j in range(srows // 16):
            parts = granule_swap(
                [recv_ref[g * n + s, 16 * j : 16 * j + 16, :].astype(f32) for s in range(n)]
            )
            for r in range(n):
                fs_ref[g, r * srows + 16 * j : r * srows + 16 * j + 16, :] = parts[r]
    row = lax.broadcasted_iota(jnp.int32, (2 * lanes, 2 * cz), 0)
    col = lax.broadcasted_iota(jnp.int32, (2 * lanes, 2 * cz), 1)
    z = col & (cz - 1)
    need = (col >> log2(cz)) * lanes + (z >> log2(zl)) * (cx * zl) + (z & (zl - 1))
    used = round_up(comps * wide, 8)
    for xi in range(cx):
        pick = jnp.where(row == need + xi * zl, 1.0, 0.0).astype(bf16)
        for pair in range(groups // 2):
            left = jnp.concatenate(
                [fs_ref[2 * pair, 0:used, :], fs_ref[2 * pair + 1, 0:used, :]], axis=1
            ).astype(bf16)
            moved = jnp.dot(left, pick, preferred_element_type=f32)
            for c in range(comps):
                out_ref[c, xi, :, 2 * cz * pair : 2 * cz * (pair + 1)] = moved[
                    c * wide : (c + 1) * wide
                ].astype(bf16)


def unpack_kernel(all_ref, in_ref, mid_a_ref, mid_b_ref, out_ref):
    rows = LAYERS * 3 * CH
    main = 8 * CH
    rest = all_ref[rows : rows + rows // 8, :]
    for k, (ref, first, count, inputs) in enumerate(
        ((in_ref, 0, CH, 3), (mid_a_ref, 0, CH, CH), (mid_b_ref, 0, CH, CH), (out_ref, 3, 6, CH))
    ):
        block = all_ref[k * 3 * CH : (k + 1) * 3 * CH, :]
        tails = []
        for half in range(2):
            j = 2 * k + half
            tails.append(pltpu.roll(rest, main - j * CH, 1) if j else rest)
        tail = jnp.concatenate(tails, axis=0)
        for dy in range(3):
            for dx in range(3):
                at = dy * 3 + dx
                if at == 8:
                    moved = tail
                else:
                    moved = pltpu.roll(block, main - at * CH, 1) if at else block
                for dz in range(3):
                    ref[(dx * 3 + dy) * 3 + dz] = moved[
                        dz * CH + first : dz * CH + first + count, 0:inputs
                    ]


def tendency(ref, x, y0, rows, forcing):
    wide = ref.shape[-1]

    def at(c, dx, dy):
        return ref[c, x + dx, y0 + 8 + dy : y0 + 8 + dy + rows, :]

    centre = [at(c, 0, 0) for c in range(3)]
    results = []
    for i in range(3):
        f0 = centre[i]
        total = None
        for j in range(3):
            if j == 0:
                m2, m1, p1, p2 = (at(i, k, 0) for k in (-2, -1, 1, 2))
            elif j == 1:
                m2, m1, p1, p2 = (at(i, 0, k) for k in (-2, -1, 1, 2))
            else:
                m2, m1, p1, p2 = (pltpu.roll(f0, (-k) % wide, 1) for k in (-2, -1, 1, 2))
            slope = 8.0 * (p1 - m1) - (p2 - m2)
            curve = 16.0 * (p1 + m1) - (p2 + m2) - 30.0 * f0
            term = viscosity * curve - centre[j] * slope
            total = term if total is None else total + term
        results.append((f0, total / 12.0 + forcing[i]))
    return results


def advance_kernel(n, v_ref, ez_ref, xl_ref, xr_ref, st_ref, idx_ref, out_ref, u_ref, f1_ref, t_ref, frc_ref):
    comps, fine_x, fine_y, fine_z = v_ref.shape
    cy = fine_y // 2
    wide = 2 * fine_z
    pad = jnp.zeros((8, wide), f32)
    rows_v = comps * fine_x * fine_y
    for c in range(comps):
        for x in range(3 * fine_x):
            u_ref[c, x, 0:8, :] = pad
            u_ref[c, x, fine_y + 8 : fine_y + 16, :] = pad
        for x in range(fine_x):
            at = slice((c * fine_x + x) * fine_y, (c * fine_x + x + 1) * fine_y)
            u_ref[c, x, 8 : fine_y + 8, 0:fine_z] = xl_ref[at, :].astype(f32)
            u_ref[c, fine_x + x, 8 : fine_y + 8, 0:fine_z] = v_ref[c, x]
            u_ref[c, 2 * fine_x + x, 8 : fine_y + 8, 0:fine_z] = xr_ref[at, :].astype(f32)
        for x in range(2 * fine_x):
            f1_ref[c, x, 0:8, :] = pad
            f1_ref[c, x, fine_y + 8 : fine_y + 16, :] = pad
    edges = jnp.concatenate(
        [
            jnp.concatenate([ref[at : at + fine_y, :], ref[at + fine_y : at + 2 * fine_y, :]], axis=1)
            for ref, at in ((xl_ref, rows_v), (ez_ref, 0), (xr_ref, rows_v))
        ],
        axis=0,
    )
    row = lax.broadcasted_iota(jnp.int32, (256, 2 * fine_z), 0)
    col = lax.broadcasted_iota(jnp.int32, (256, 2 * fine_z), 1)
    lane = col & (fine_z - 1)
    for c in range(comps):
        for x in range(0, fine_x, 2):
            base = (c * fine_x + x) * 8 + (col >> log2(fine_z)) * 8
            need = jnp.where(lane < 4, 128 + base + lane, base + lane - (fine_z - 8))
            hit = (row == need) & ((lane < 4) | (lane >= fine_z - 4))
            moved = jnp.dot(
                edges, jnp.where(hit, 1.0, 0.0).astype(bf16), preferred_element_type=f32
            )
            for s in range(3):
                for e in range(2):
                    u_ref[c, s * fine_x + x + e, 8 : fine_y + 8, fine_z:wide] = moved[
                        s * fine_y : (s + 1) * fine_y, e * fine_z : (e + 1) * fine_z
                    ]

    half_lane = lax.broadcasted_iota(jnp.int32, (3 * cy, 128), 1) < 64
    lows, highs = [], []
    for s in range(0, n, 2):
        a, b = st_ref[s].astype(f32), st_ref[s + 1].astype(f32)
        lows.append(jnp.where(half_lane, a, pltpu.roll(b, 64, 1)).astype(bf16))
        highs.append(jnp.where(half_lane, pltpu.roll(a, 64, 1), b).astype(bf16))
    low = jnp.concatenate(lows, axis=1)
    high = jnp.concatenate(highs, axis=1)
    row = lax.broadcasted_iota(jnp.int32, (64 * n, wide), 0)
    for k in range(6):
        pick = jnp.where(row == idx_ref[k], 1.0, 0.0).astype(bf16)
        for h, src in enumerate((low, high)):
            moved = jnp.dot(src, pick, preferred_element_type=f32)
            for c in range(3):
                t_ref[3 * h + c, k, 0:8, :] = pad
                t_ref[3 * h + c, k, cy + 8 : cy + 16, :] = pad
                t_ref[3 * h + c, k, 8 : cy + 8, :] = moved[c * cy : (c + 1) * cy]

    scale = -closure_weight / 12.0

    def force(kk, carry):
        k = kk + 1
        for y0 in range(0, cy, 8):
            for i in range(3):
                ax, ay, az = pair_table[i]
                tz = t_ref[az, k, y0 + 8 : y0 + 16, :]
                m2, m1, p1, p2 = (pltpu.roll(tz, (-e) % wide, 1) for e in (-2, -1, 1, 2))
                along_z = 8.0 * (p1 - m1) - (p2 - m2)
                m, o, p = (t_ref[ay, k, y0 + 8 + e : y0 + 16 + e, :] for e in (-1, 0, 1))
                even = along_z + (8.0 * o - 7.0 * m - p)
                odd = along_z + (7.0 * p - 8.0 * o + m)
                m, o, p = (t_ref[ax, k + e, y0 + 8 : y0 + 16, :] for e in (-1, 0, 1))
                for px in range(2):
                    along_x = 7.0 * p - 8.0 * o + m if px else 8.0 * o - 7.0 * m - p
                    for py, part in enumerate((even, odd)):
                        value = scale * (along_x + part)
                        for h in range(0, wide, 128):
                            frc_ref[
                                h // 128, i, 2 * kk + px, pl.ds(2 * y0 + py, 8, stride=2), :
                            ] = value[:, h : h + 128]
        return carry

    lax.fori_loop(0, fine_x, force, 0)

    def forcing_at(x, y0):
        return [
            jnp.concatenate(
                [frc_ref[h, i, x, y0 : y0 + rows, :] for h in range(wide // 128)], axis=1
            )
            for i in range(3)
        ]

    rows = 8

    def one(x, carry):
        for y0 in range(0, fine_y, rows):
            for i, (f0, t) in enumerate(tendency(u_ref, x + 2, y0, rows, forcing_at(x, y0))):
                f1_ref[i, x, y0 + 8 : y0 + 8 + rows, :] = f0 + step_size * t
        return carry

    lax.fori_loop(0, 2 * fine_x, one, 0)

    def two(x, carry):
        for y0 in range(0, fine_y, rows):
            for i, (f0, t) in enumerate(tendency(f1_ref, x + 2, y0, rows, forcing_at(x + 2, y0))):
                nxt = (f0 + step_size * t)[:, 0:fine_z]
                out_ref[i, x, y0 : y0 + rows, :] = 0.5 * (v_ref[i, x, y0 : y0 + rows, :] + nxt)
        return carry

    lax.fori_loop(0, fine_x, two, 0)


def send_table(n, hops, cx, zl, lanes):
    nt = 2 * hops + 1
    total_x = n * cx
    window = zl + 2
    table = np.full((2, n // 2, 1, 256), -1, np.int32)
    for variant in range(2):
        z0 = -2 if variant == 0 else 0
        for d in range(n):
            for half in range(2):
                for xk in range(cx + 4):
                    for e in range(window):
                        x = (cx * d - 2 + xk) % total_x
                        z = z0 + e
                        t, zp = hops + z // zl, z % zl
                        src = half * nt * lanes + t * lanes + x * zl + zp
                        lane = half * 64 + xk * window + e
                        table[variant, d // 2, 0, (d % 2) * 128 + lane] = src
    return table


def spread_table(n, cx, zl, fine_z):
    window = zl + 2
    cz = fine_z // 2
    table = np.full((cx + 4, 1, 2 * fine_z), -1, np.int32)
    for k in range(cx + 4):
        for lane in range(2 * fine_z):
            if lane < fine_z + 4:
                z = lane // 2
            elif lane >= 2 * fine_z - 4:
                z = (lane - 2 * fine_z) // 2
            else:
                continue
            s = min(max(z // zl, 0), n - 1)
            z0 = -2 if s < n // 2 else 0
            table[k, 0, lane] = s * 64 + k * window + (z - s * zl - z0)
    return table


def local(velocity, w_in, w_mid_a, w_mid_b, w_out):
    n = lax.axis_size("slab")
    groups = lax.axis_size("grp")
    devices = n * groups
    comps, fine_x, fine_y, fine_z = velocity.shape
    cx, cy, cz = fine_x // 2, fine_y // 2, fine_z // 2
    zl = cz // n
    lanes = n * cx * zl
    hops = -(-MARGIN // zl)
    nt = 2 * hops + 1
    assert lanes == 128 and fine_z == 128 and cx == 2 and cy % 8 == 0 and (cx + 4) * (zl + 2) <= 64
    length = 6 * n * cx * cy * groups * cz
    both = ("grp", "slab")

    def ring(x, shift):
        return lax.ppermute(x, both, [(i, (i + shift) % devices) for i in range(devices)])

    def shift(x, axis, by):
        count = lax.axis_size(axis)
        return lax.ppermute(x, axis, [(i, (i + by) % count) for i in range(count)])

    spread = jnp.stack(
        [
            jnp.pad(w_in, ((0, 0), (0, 0), (0, CH - 3))),
            w_mid_a,
            w_mid_b,
            jnp.pad(w_out, ((0, 0), (3, CH - 9), (0, 0))),
        ]
    ).reshape(LAYERS, 3, 3, 3, CH, CH)
    w_fwd = jnp.transpose(spread, (0, 3, 4, 2, 1, 5)).reshape(LAYERS, 3 * CH, 9 * CH)
    w_bwd = jnp.transpose(spread[:, ::-1, ::-1, ::-1], (0, 3, 5, 2, 1, 4)).reshape(
        LAYERS, 3 * CH, 9 * CH
    )

    group = round_up(-(-9 * cy // n), 16)
    fields = call(
        functools.partial(filter_kernel, n),
        jax.ShapeDtypeStruct((n, group, lanes), bf16),
        [pltpu.VMEM((9 * cy, cx * fine_z), f32), pltpu.VMEM((n * group, lanes), f32)],
        4_000_000_000,
        1,
    )(velocity)
    mine = lax.all_to_all(fields, "slab", 0, 0, tiled=True)

    v16, edge = call(
        edge_kernel,
        (
            jax.ShapeDtypeStruct((comps * fine_x * fine_y, fine_z), bf16),
            jax.ShapeDtypeStruct((fine_y, 128), bf16),
        ),
        [],
        1_000_000_000,
        1,
    )(velocity)
    from_left = shift(edge, "grp", 1)
    from_right = shift(edge, "grp", -1)
    edges = jnp.concatenate([from_left, from_right], axis=0)

    lower = [ring(mine, k) for k in range(hops, 0, -1)]
    upper = [ring(mine, -k) for k in range(1, hops + 1)]
    edges, v16, lower, upper = lax.optimization_barrier((edges, v16, lower, upper))
    pack = jnp.concatenate([v16, edges], axis=0)
    pack_left = shift(pack, "slab", 1)
    pack_right = shift(pack, "slab", -1)

    place = lax.axis_index("slab")
    tables = send_table(n, hops, cx, zl, lanes)
    send_idx = jnp.where(place < n // 2, tables[0], tables[1])
    srows = round_up(-(-6 * (cy // groups) // n), 16)
    grad_rows = LAYERS * 3 * CH * 9 // 8
    per_device = round_up(-(-grad_rows // devices), 8)
    act = pltpu.VMEM((cy + 2, 3 * CH, nt * lanes), bf16)
    bsend, ssend, grads = call(
        functools.partial(
            closure_kernel, (n, hops, groups, devices, cy, cx, zl, length)
        ),
        (
            jax.ShapeDtypeStruct((n, 3 * cy, 128), bf16),
            jax.ShapeDtypeStruct((devices, srows, lanes), bf16),
            jax.ShapeDtypeStruct((devices * per_device, 128), f32),
        ),
        [
            act,
            act,
            act,
            act,
            act,
            pltpu.VMEM((cy, 3 * CH, lanes), bf16),
            pltpu.VMEM((nt, max(CH * cy, n * group), lanes), f32),
            pltpu.VMEM((n * srows, lanes), f32),
            pltpu.VMEM((LAYERS, 3 * CH, 9 * CH), f32),
        ],
        40_000_000_000,
        nt + 3,
    )(*lower, mine, *upper, w_fwd, w_bwd, send_idx)

    st = lax.all_to_all(bsend, "slab", 0, 0, tiled=True)
    partial_sums = lax.all_to_all(
        grads.reshape(devices, per_device, 128), both, 0, 0, tiled=True
    )
    total = jnp.sum(partial_sums, axis=0)
    summed = lax.all_to_all(
        jnp.broadcast_to(total[None], (devices, per_device, 128)), both, 0, 0, tiled=True
    ).reshape(devices * per_device, 128)
    out_blocks = lax.all_to_all(ssend, both, 0, 0, tiled=True)

    velocity_next = call(
        functools.partial(advance_kernel, n),
        jax.ShapeDtypeStruct(velocity.shape, f32),
        [
            pltpu.VMEM((comps, 3 * fine_x, fine_y + 16, 2 * fine_z), f32),
            pltpu.VMEM((comps, 2 * fine_x, fine_y + 16, 2 * fine_z), f32),
            pltpu.VMEM((6, cx + 4, cy + 16, 2 * fine_z), f32),
            pltpu.VMEM((2 * fine_z // 128, comps, 2 * fine_x, fine_y, 128), f32),
        ],
        15_000_000_000,
        6,
    )(velocity, edges, pack_left, pack_right, st, spread_table(n, cx, zl, fine_z))

    stress = call(
        functools.partial(stress_kernel, n, groups, zl),
        jax.ShapeDtypeStruct((6, cx, cy // groups, groups * cz), bf16),
        [pltpu.VMEM((groups, n * srows, lanes), f32)],
        1_000_000_000,
        1,
    )(out_blocks)
    grad_in, grad_mid_a, grad_mid_b, grad_out = call(
        unpack_kernel,
        (
            jax.ShapeDtypeStruct((27, CH, 3), f32),
            jax.ShapeDtypeStruct((27, CH, CH), f32),
            jax.ShapeDtypeStruct((27, CH, CH), f32),
            jax.ShapeDtypeStruct((27, 6, CH), f32),
        ),
        [],
        1_000_000_000,
        1,
    )(summed)
    return (velocity_next, stress, grad_in, grad_mid_a, grad_mid_b, grad_out)


def solution(mesh):
    in_specs = (P(None, "slab", None, "grp"), P(), P(), P(), P())
    out_specs = (P(None, "slab", None, "grp"), P(None, "slab", "grp", None), P(), P(), P(), P())
    return jax.shard_map(local, mesh=mesh, in_specs=in_specs, out_specs=out_specs, check_vma=False)
```

time: 987 us -> 307 us (0.31); the launches traced: 973 us -> 306 us
  local copies, waits for them, and re-layouts: 518 us -> 14.2 us
  Pallas kernels: 0 us -> 214 us
  waiting for transfers between devices: 169 us -> 29.4 us
  other arithmetic: 124 us -> 0.77 us
  matrix products: 77.3 us -> 0 us
  starting transfers between devices: 68.2 us -> 25.5 us
  blocking collectives: 0 us -> 22 us
  between operations: 15.9 us -> 0.81 us
    pallas_call x0 -> x6, Pallas kernels: none -> 214 us  [the longest x1 186 us: local(): call(functools.partial(closure_kernel, (n, hops, groups, devices, cy, cx,...]
    reshape x59 -> x2, local copies, waits for them, and re-layouts: 161 us -> 1.89 us  [the longest x1 0.95 us: local(): jnp.transpose(spread, (0, 3, 4, 2, 1, 5)).reshape(LAYERS, 3 * CH, 9 * CH)]
    another operation x19 -> x0, local copies, waits for them, and re-layouts: 136 us -> none  [the longest x7 129 us: filter_fields(): jnp.stack([velocity[left_comp] * velocity[right_comp] for left_comp, righ...]
    psum x1 -> x0, waiting for transfers between devices: 118 us -> none  [local(): lax.psum((gradients[0], gradients[1], gradients[2], gradients[3]), ('grp'...]
    unnamed x234 -> x46, local copies, waits for them, and re-layouts: 123 us -> 11.4 us
    dot_general x33 -> x0, matrix products: 77.3 us -> none  [the longest x12 42.5 us: weight_gradient(): lax.dot_general(moved, columns, (((1,), (1,)), ((), ())), preferred_eleme...]
    slice x56 -> x0, local copies, waits for them, and re-layouts: 55.8 us -> none  [the longest x22 33.2 us: convolve(): summed = summed + jnp.roll(partial_value, 1 - shift_z, axis=3)]
    reduce_sum x2 -> x1, other arithmetic: 52.2 us -> 0.04 us  [local(): total = jnp.sum(partial_sums, axis=0)]
  transfers between devices with their start and end apart: 39 -> 9, of which waited for: 13 -> 6; matrix products, arithmetic and copies ran while one was open for 24% -> 3% of each run, Pallas kernels for 0% -> 3%
where the time goes in v1:
time: 307 us; the launch traced here: 306 us
  Pallas kernels  214 us (70%)
  waiting for transfers between devices  29.4 us (10%)
  starting transfers between devices  25.5 us (8%)
  blocking collectives  22 us (7%)
  local copies, waits for them, and re-layouts  14.2 us (5%)
    pallas_call x1, Pallas kernels, local(): call(functools.partial(closure_kernel, (n, hops, groups, devices, cy, cx,...  186 us
    pallas_call x1, Pallas kernels, local(): call(functools.partial(advance_kernel, n), jax.ShapeDtypeStruct(velocity....  17 us
    ppermute x4, waiting for transfers between devices, shift(): return lax.ppermute(x, axis, [(i, (i + by) % count) for i in range(count)])  15.3 us
    all_to_all x1, blocking collectives, local(): lax.all_to_all(grads.reshape(devices, per_device, 128), both, 0, 0, tiled...  11.8 us
    unnamed x46, local copies, waits for them, and re-layouts  11.4 us
    all_to_all x1, blocking collectives, local(): lax.all_to_all(jnp.broadcast_to(total[None], (devices, per_device, 128)),...  10.2 us
    all_to_all x1, waiting for transfers between devices, local(): out_blocks = lax.all_to_all(ssend, both, 0, 0, tiled=True)  7.77 us
    ppermute x4, starting transfers between devices, shift(): return lax.ppermute(x, axis, [(i, (i + by) % count) for i in range(count)])  7.21 us
  transfers between devices with their start and end apart: 9, of which 6 were waited for; matrix products, arithmetic and copies ran while one was open for 3% of the time, Pallas kernels for 3%

profile of v1, /device:TPU:0, one launch (start us, length us, event | category | flops | bytes accessed | tf_op | source)
XLA Modules:
  0.0 306.1 jit_solution(833922709092285628)
XLA Ops:
  0.6 2.2 shard_map.127
  2.8 0.5 collective-permute-start
  3.3 1.9 collective-permute-start.1
  5.2 4.1 %shard_map.128 = bf16[8,96,128]{2,1,0:T(8,128)(2,1)} custom-call(f32[3,4,144,128]{3,2,1,0:T(8,128)} %v_ref.5), custom_call_target="tpu_custom_call" | custom-call | flops 4000000000 | bytes 10000000 | tf_op jit(solution)/shard_map/pallas_call | solution.py:600
  9.3 6.7 %all-to-all-start = ((bf16[8,96,128]{2,1,0:T(8,128)(2,1)}), bf16[8,96,128]{2,1,0:T(8,128)(2,1)S(1)}, u32[]{:S(2)}, u32[]{:S(2)}) async-start(bf16[8,96,128]{2,1,0:T(8,128)(2,1)} %shard_map.128), calls=%async_computation | async-start | bytes 393216 | tf_op jit(solution)/shard_map/all_to_all | solution.py:607
  16.1 0.0 copy-done.11
  16.1 0.0 copy-start.10
  16.1 0.2 copy.24
  16.3 0.5 copy-done.10
  16.8 0.1 copy.27
  17.0 0.0 copy-start.8
  17.0 0.8 copy-done.8
  17.8 0.2 copy.25
  18.0 0.6 copy-done.9
  18.7 0.2 copy.26
  18.9 0.0 copy-start.12
  18.9 0.0 copy-start.13
  18.9 0.1 pad_maximum_fusion
  19.0 0.5 copy-done.12
  19.6 0.0 copy-done.13
  19.6 0.6 broadcast_select_fusion.refs_5_
  20.2 3.9 %all-to-all-done.refs_1_ = bf16[8,96,128]{2,1,0:T(8,128)(2,1)S(1)} async-done(((bf16[8,96,128]{2,1,0:T(8,128)(2,1)}), bf16[8,96,128]{2,1,0:T(8,128)(2,1)S(1)}, u32[]{:S(2)}, u32[]{:S(2)}) %all-to-all-start) | async-done | bytes 196640 | tf_op jit(solution)/shard_map/all_to_all | solution.py:607
  24.1 1.0 collective-permute-start.2
  25.1 4.3 %collective-permute-start.3 = (bf16[8,96,128]{2,1,0:T(8,128)(2,1)S(1)}, bf16[8,96,128]{2,1,0:T(8,128)(2,1)S(1)}, u32[]{:S(2)}, u32[]{:S(2)}) collective-permute-start(bf16[8,96,128]{2,1,0:T(8,128)(2,1)S(1)} %all-to-all-done.refs_1_), channel_id=1, source_target_pairs={{0,31},{1,0},{2,1},{3,2},{4,3},{5,4},{6,5},{7,6},{8,7},{9,8},{10,9... | collective-permute-start | bytes 589832 | tf_op jit(solution)/shard_map/ppermute | solution.py:580
  29.4 0.0 copy-done.5
  29.5 0.5 copy.29
  29.9 0.9 reshape.35.refs_4_
  30.9 0.3 copy.28
  31.1 0.9 reshape.34.refs_3_
  32.1 0.0 collective-permute-done
  32.1 0.0 collective-permute-done.1
  32.1 0.0 copy-start.2
  32.1 0.7 collective-permute-done.2.refs_0_
  32.8 1.7 collective-permute-done.3.refs_2_
  34.5 0.0 copy-done.16
  34.5 0.7 copy-done.17
  35.2 186.4 %shard_map.129 = (bf16[8,216,128]{2,1,0:T(8,128)(2,1)}, bf16[32,16,128]{2,1,0:T(8,128)(2,1)}, f32[256,128]{1,0:T(8,128)}) custom-call(bf16[8,96,128]{2,1,0:T(8,128)(2,1)} %copy-done.16, bf16[8,96,128]{2,1,0:T(8,128)(2,1)} %copy-done.5, bf16[8,96,128]{2,1,0:T(8,128)(2,1)} %copy-done.17, bf16[4,48,144]{2,1,0:T(8,128)(2,1)} %reshape.34.refs_3_, ...), custom_call_target="tpu_custom_call" | custom-call | flops 40000000000 | bytes 100000000 | tf_op jit(solution)/shard_map/pallas_call | solution.py:637
  221.6 11.8 %all_to_all.25 = f32[32,8,128]{2,1,0:T(8,128)S(1)} all-to-all(f32[32,8,128]{2,1,0:T(8,128)} %bitcast.15), channel_id=1, replica_groups=mesh['grp'=4,'slab'=8] {'grp','slab'}, dimensions={0} | all-to-all | bytes 262144 | tf_op jit(solution)/shard_map/all_to_all | solution.py:662
  233.3 2.6 all-to-all-start.2
  236.0 7.8 %all-to-all-done.2.recv_ref = bf16[32,16,128]{2,1,0:T(8,128)(2,1)S(1)} async-done(((bf16[32,16,128]{2,1,0:T(8,128)(2,1)}), bf16[32,16,128]{2,1,0:T(8,128)(2,1)S(1)}, u32[]{:S(2)}, u32[]{:S(2)}) %all-to-all-start.2) | async-done | bytes 131104 | tf_op jit(solution)/shard_map/all_to_all | solution.py:669
  243.8 10.2 %all_to_all.26 = f32[32,8,128]{2,1,0:T(8,128)} all-to-all(f32[32,8,128]{2,1,0:T(8,128)S(1)} %broadcast_in_dim.2), channel_id=1, replica_groups=mesh['grp'=4,'slab'=8] {'grp','slab'}, dimensions={0} | all-to-all | bytes 262144 | tf_op jit(solution)/shard_map/all_to_all | solution.py:666
  253.9 0.0 copy-done.6
  254.0 3.6 %all-to-all-start.1 = ((bf16[8,216,128]{2,1,0:T(8,128)(2,1)}), bf16[8,216,128]{2,1,0:T(8,128)(2,1)S(1)}, u32[]{:S(2)}, u32[]{:S(2)}) async-start(bf16[8,216,128]{2,1,0:T(8,128)(2,1)} %get-tuple-element.25), calls=%async_computation.1 | async-start | bytes 884736 | tf_op jit(solution)/shard_map/all_to_all | solution.py:661
  257.6 0.0 copy-done
  257.6 0.0 copy-done.2
  257.6 2.0 collective-permute-start.4
  259.6 2.8 collective-permute-start.5
  262.4 2.0 shard_map.131
  264.4 1.6 copy.30
  266.0 1.9 shard_map.132
  267.9 1.8 copy.32
  269.7 0.0 copy-done.4
  269.7 0.8 copy.33
  270.5 0.1 copy-done.7
  270.6 0.7 copy.34
  271.3 0.0 copy-done.3
  271.3 0.8 copy.31
  272.2 13.0 %collective-permute-done.4.xl_ref = bf16[2016,128]{1,0:T(8,128)(2,1)S(1)} collective-permute-done((bf16[2016,128]{1,0:T(8,128)(2,1)S(1)}, bf16[2016,128]{1,0:T(8,128)(2,1)S(1)}, u32[]{:S(2)}, u32[]{:S(2)}) %collective-permute-start.4) | collective-permute-done | bytes 516128 | tf_op jit(solution)/shard_map/ppermute | solution.py:584
  285.1 2.4 collective-permute-done.5.xr_ref
  287.5 0.0 all-to-all-done.1.st_ref
  287.5 0.0 copy-done.14
  287.5 0.8 copy-done.15
  288.3 0.8 copy-done.1
  289.1 17.0 %shard_map.130 = f32[3,4,144,128]{3,2,1,0:T(8,128)} custom-call(f32[3,4,144,128]{3,2,1,0:T(8,128)} %v_ref.5, bf16[288,128]{1,0:T(8,128)(2,1)} %copy-done.2, bf16[2016,128]{1,0:T(8,128)(2,1)} %copy-done.14, bf16[2016,128]{1,0:T(8,128)(2,1)} %copy-done.15, bf16[8,216,128]{2,1,0:T(8,128)(2,1)} %copy-done.1, s32[6,1,256]{2,1,0:T(1,128)} %constant.19.clone.idx_ref), custom_call_target="tpu_custom_call" | custom-call | flops 15000000512 | bytes 37500000 | tf_op jit(solution)/shard_map/pallas_call | solution.py:671
  (21 shorter events, 0.2 us)
Async XLA Ops:
  2.8 29.3 %collective-permute-start = (bf16[144,128]{1,0:T(8,128)(2,1)}, bf16[144,128]{1,0:T(8,128)(2,1)S(1)}, u32[]{:S(2)}, u32[]{:S(2)}) collective-permute-start(bf16[144,128]{1,0:T(8,128)(2,1)} %get-tuple-element.19), channel_id=1, source_target_pairs={{0,8},{8,16},{16,24},{24,0},{1,9},{9,17},{17,25},{25,1},{2,10},{10... | collective-permute-start | bytes 110600 | tf_op jit(solution)/shard_map/ppermute | solution.py:584
  3.3 28.8 %collective-permute-start.1 = (bf16[144,128]{1,0:T(8,128)(2,1)}, bf16[144,128]{1,0:T(8,128)(2,1)S(1)}, u32[]{:S(2)}, u32[]{:S(2)}) collective-permute-start(bf16[144,128]{1,0:T(8,128)(2,1)} %get-tuple-element.19), channel_id=1, source_target_pairs={{0,24},{8,0},{16,8},{24,16},{1,25},{9,1},{17,9},{25,17},{2,26},{10... | collective-permute-start | bytes 110600 | tf_op jit(solution)/shard_map/ppermute | solution.py:584
  9.3 6.7 %copy-start.11 = (bf16[27,16,3]{0,1,2:T(8,128)(2,1)S(1)}, bf16[27,16,3]{0,1,2:T(8,128)(2,1)}, u32[]{:S(2)}) copy-start(bf16[27,16,3]{0,1,2:T(8,128)(2,1)} %param.9) | copy-start | bytes 7780
  9.3 14.7 %all-to-all-start = ((bf16[8,96,128]{2,1,0:T(8,128)(2,1)}), bf16[8,96,128]{2,1,0:T(8,128)(2,1)S(1)}, u32[]{:S(2)}, u32[]{:S(2)}) async-start(bf16[8,96,128]{2,1,0:T(8,128)(2,1)} %shard_map.128), calls=%async_computation | async-start | bytes 393216 | tf_op jit(solution)/shard_map/all_to_all | solution.py:607
  16.1 0.7 copy-start.10
  17.0 0.8 copy-start.8
  17.8 0.8 copy-start.9
  18.9 0.7 copy-start.12
  18.9 0.7 copy-start.13
  24.1 5.4 %copy-start.5 = (bf16[8,96,128]{2,1,0:T(8,128)(2,1)}, bf16[8,96,128]{2,1,0:T(8,128)(2,1)S(1)}, u32[]{:S(2)}) copy-start(bf16[8,96,128]{2,1,0:T(8,128)(2,1)S(1)} %all-to-all-done.refs_1_) | copy-start | bytes 589828
  24.1 8.7 %collective-permute-start.2 = (bf16[8,96,128]{2,1,0:T(8,128)(2,1)S(1)}, bf16[8,96,128]{2,1,0:T(8,128)(2,1)S(1)}, u32[]{:S(2)}, u32[]{:S(2)}) collective-permute-start(bf16[8,96,128]{2,1,0:T(8,128)(2,1)S(1)} %all-to-all-done.refs_1_), channel_id=1, source_target_pairs={{0,1},{1,2},{2,3},{3,4},{4,5},{5,6},{6,7},{7,8},{8,9},{9,10},{10,1... | collective-permute-start | bytes 589832 | tf_op jit(solution)/shard_map/ppermute | solution.py:580
  25.1 9.4 %collective-permute-start.3 = (bf16[8,96,128]{2,1,0:T(8,128)(2,1)S(1)}, bf16[8,96,128]{2,1,0:T(8,128)(2,1)S(1)}, u32[]{:S(2)}, u32[]{:S(2)}) collective-permute-start(bf16[8,96,128]{2,1,0:T(8,128)(2,1)S(1)} %all-to-all-done.refs_1_), channel_id=1, source_target_pairs={{0,31},{1,0},{2,1},{3,2},{4,3},{5,4},{6,5},{7,6},{8,7},{9,8},{10,9... | collective-permute-start | bytes 589832 | tf_op jit(solution)/shard_map/ppermute | solution.py:580
  32.1 225.5 %copy-start.2 = (bf16[288,128]{1,0:T(8,128)(2,1)}, bf16[288,128]{1,0:T(8,128)(2,1)S(1)}, u32[]{:S(2)}) copy-start(bf16[288,128]{1,0:T(8,128)(2,1)S(1)} %pad_maximum_fusion.1.ez_ref) | copy-start | bytes 221188
  32.8 1.7 copy-start.16
  34.5 0.7 copy-start.17
  233.3 10.4 %all-to-all-start.2 = ((bf16[32,16,128]{2,1,0:T(8,128)(2,1)}), bf16[32,16,128]{2,1,0:T(8,128)(2,1)S(1)}, u32[]{:S(2)}, u32[]{:S(2)}) async-start(bf16[32,16,128]{2,1,0:T(8,128)(2,1)} %get-tuple-element.26), calls=%async_computation.2 | async-start | bytes 262144 | tf_op jit(solution)/shard_map/all_to_all | solution.py:669
  243.7 10.2 %copy-start.6 = (bf16[32,16,128]{2,1,0:T(8,128)(2,1)}, bf16[32,16,128]{2,1,0:T(8,128)(2,1)S(1)}, u32[]{:S(2)}) copy-start(bf16[32,16,128]{2,1,0:T(8,128)(2,1)S(1)} %all-to-all-done.2.recv_ref) | copy-start | bytes 393220
  253.9 3.6 %copy-start = (bf16[1728,128]{1,0:T(8,128)(2,1)S(1)}, bf16[1728,128]{1,0:T(8,128)(2,1)}, u32[]{:S(2)}) copy-start(bf16[1728,128]{1,0:T(8,128)(2,1)} %get-tuple-element.22) | copy-start | bytes 1327108
  254.0 33.5 %all-to-all-start.1 = ((bf16[8,216,128]{2,1,0:T(8,128)(2,1)}), bf16[8,216,128]{2,1,0:T(8,128)(2,1)S(1)}, u32[]{:S(2)}, u32[]{:S(2)}) async-start(bf16[8,216,128]{2,1,0:T(8,128)(2,1)} %get-tuple-element.25), calls=%async_computation.1 | async-start | bytes 884736 | tf_op jit(solution)/shard_map/all_to_all | solution.py:661
  257.6 27.5 %collective-permute-start.4 = (bf16[2016,128]{1,0:T(8,128)(2,1)S(1)}, bf16[2016,128]{1,0:T(8,128)(2,1)S(1)}, u32[]{:S(2)}, u32[]{:S(2)}) collective-permute-start(bf16[2016,128]{1,0:T(8,128)(2,1)S(1)} %constant_dynamic-update-slice_fusion), channel_id=1, source_target_pairs={{0,1},{1,2},{2,3},{3,4},{4,5},{5,6},{6,7},{7,0},{8,9},{9,10},{10,1... | collective-permute-start | bytes 1548296 | tf_op jit(solution)/shard_map/ppermute | solution.py:584
  259.6 27.9 %collective-permute-start.5 = (bf16[2016,128]{1,0:T(8,128)(2,1)S(1)}, bf16[2016,128]{1,0:T(8,128)(2,1)S(1)}, u32[]{:S(2)}, u32[]{:S(2)}) collective-permute-start(bf16[2016,128]{1,0:T(8,128)(2,1)S(1)} %constant_dynamic-update-slice_fusion), channel_id=1, source_target_pairs={{0,7},{1,0},{2,1},{3,2},{4,3},{5,4},{6,5},{7,6},{8,15},{9,8},{10,9... | collective-permute-start | bytes 1548296 | tf_op jit(solution)/shard_map/ppermute | solution.py:584
  267.9 1.8 copy-start.4
  269.7 0.9 copy-start.7
  269.7 1.6 copy-start.3
  285.1 2.4 copy-start.14
  287.5 0.8 copy-start.15
  288.3 0.8 copy-start.1

commit v2 on v1

--- a/solution.py
+++ b/solution.py
@@ -18,7 +18,8 @@
 MARGIN = LAYERS + LAYERS - 1
 f32 = jnp.float32
 bf16 = jnp.bfloat16
-VMEM_LIMIT = 60 * 1024 * 1024
+BATCH = 8
+MIB = 1024 * 1024
 
 
 def round_up(a, b):
@@ -30,8 +31,13 @@
     return n.bit_length() - 1
 
 
+def nbytes(shapes):
+    return sum(int(np.prod(x.shape)) * jnp.dtype(x.dtype).itemsize for x in shapes)
+
+
 def call(body, out_shape, scratch, cost, n_in):
     many = isinstance(out_shape, (tuple, list))
+    grant = max(36 * MIB, min(62 * MIB, int(1.1 * nbytes(scratch)) + 9 * MIB))
     spec = pl.BlockSpec(memory_space=pltpu.VMEM)
     return pl.pallas_call(
         body,
@@ -39,7 +45,7 @@
         in_specs=[spec] * n_in,
         out_specs=[spec] * len(out_shape) if many else spec,
         scratch_shapes=scratch,
-        compiler_params=pltpu.CompilerParams(vmem_limit_bytes=VMEM_LIMIT),
+        compiler_params=pltpu.CompilerParams(vmem_limit_bytes=grant),
         cost_estimate=pl.CostEstimate(flops=cost, bytes_accessed=cost // 400, transcendentals=0),
     )
 
@@ -68,7 +74,7 @@
 
 
 def filter_kernel(n, v_ref, out_ref, q_ref, f_ref):
-    comps, fine_x, fine_y, fine_z = v_ref.shape
+    _, fine_x, fine_y, fine_z = v_ref.shape
     cx, cy, cz = fine_x // 2, fine_y // 2, fine_z // 2
     zl = cz // n
     group = out_ref.shape[1]
@@ -141,13 +147,14 @@
 
 
 def closure_kernel(dims, *refs):
-    n, hops, groups, devices, cy, cx, zl, length = dims
+    n, hops, groups, _, cy, _, zl, length = dims
     nt = 2 * hops + 1
     tiles = refs[:nt]
     wf_ref, wb_ref, idx_ref = refs[nt : nt + 3]
     bsend_ref, ssend_ref, grad_ref = refs[nt + 3 : nt + 6]
     acts = refs[nt + 6 : nt + 10]
     cot_ref, cz_ref, f_ref, fs_ref, g_ref = refs[nt + 10 :]
+    unroll = max(u for u in range(1, cy + 1) if cy % u == 0 and u * nt <= 36)
     group = tiles[0].shape[1]
     lanes = tiles[0].shape[2]
     own = hops * lanes
@@ -185,13 +192,23 @@
         cz_ref[y, CH : 2 * CH, :] = tile(value, hops).astype(bf16)
         cz_ref[y, 2 * CH : 3 * CH, :] = before(value, hops).astype(bf16)
 
-    def convolve(src, w, y):
-        columns = src[pl.ds(y, 3)].reshape(9 * CH, nt * lanes)
-        parts = jnp.dot(w, columns, preferred_element_type=f32)
-        low, mid, high = parts[0:CH], parts[CH : 2 * CH], parts[2 * CH :]
-        return jnp.concatenate(
-            [tile(mid, t) + before(low, t) + after(high, t) for t in range(nt)], axis=1
-        )
+    def convolve(src, w, ys):
+        results = []
+        for y in ys:
+            columns = src[pl.ds(y, 3)].reshape(9 * CH, nt * lanes)
+            results.append(jnp.dot(w, columns, preferred_element_type=f32))
+        sums = []
+        for parts in results:
+            low, mid, high = parts[0:CH], parts[CH : 2 * CH], parts[2 * CH :]
+            sums.append(
+                jnp.concatenate(
+                    [tile(mid, t) + before(low, t) + after(high, t) for t in range(nt)], axis=1
+                )
+            )
+        return sums
+
+    def rows_at(j):
+        return [unroll * j + u for u in range(unroll)]
 
     for ref in (*acts, cot_ref):
         zero = jnp.zeros((3 * CH, nt * lanes), bf16)
@@ -214,54 +231,61 @@
     def load_fields(y):
         return jnp.concatenate([f_ref[t, pl.ds(y, CH, stride=cy), :] for t in range(nt)], axis=1)
 
-    def start(y, carry):
-        put(acts[0], y, load_fields(y))
+    def start(j, carry):
+        for y in rows_at(j):
+            put(acts[0], y, load_fields(y))
         return carry
 
-    lax.fori_loop(0, cy, start, 0)
+    lax.fori_loop(0, cy // unroll, start, 0)
 
     for k in range(LAYERS - 1):
         w = wf_ref[k]
 
-        def forward(y, carry, k=k, w=w):
-            put(acts[k + 1], y, jnp.tanh(convolve(acts[k], w, y)))
+        def forward(j, carry, k=k, w=w):
+            ys = rows_at(j)
+            outs = [jnp.tanh(v) for v in convolve(acts[k], w, ys)]
+            for y, v in zip(ys, outs):
+                put(acts[k + 1], y, v)
             return carry
 
-        lax.fori_loop(0, cy, forward, 0)
+        lax.fori_loop(0, cy // unroll, forward, 0)
 
     w_last = wf_ref[LAYERS - 1]
     channel = lax.broadcasted_iota(jnp.int32, (CH, nt * lanes), 0)
     stressed = (channel >= 3) & (channel < 9)
 
-    def predict(y, carry):
-        predicted = convolve(acts[LAYERS - 1], w_last, y)
-        target = load_fields(y)
-        cot = jnp.where(stressed, 2.0 / length * (predicted - target), 0.0)
-        put(cot_ref, y, cot)
-        put_cz(y, cot)
-        stress = rounded(predicted)
-        for t in range(nt):
-            f_ref[t, pl.ds(y, CH, stride=cy), :] = tile(stress, t)
+    def predict(j, carry):
+        ys = rows_at(j)
+        targets = [load_fields(y) for y in ys]
+        predicted = convolve(acts[LAYERS - 1], w_last, ys)
+        cots = [
+            jnp.where(stressed, 2.0 / length * (v - target), 0.0)
+            for v, target in zip(predicted, targets)
+        ]
+        for y, cot in zip(ys, cots):
+            put(cot_ref, y, cot)
+            put_cz(y, cot)
+        for y, v in zip(ys, predicted):
+            stress = rounded(v)
+            for t in range(nt):
+                f_ref[t, pl.ds(y, CH, stride=cy), :] = tile(stress, t)
         return carry
 
-    lax.fori_loop(0, cy, predict, 0)
+    lax.fori_loop(0, cy // unroll, predict, 0)
 
     def weight_gradient(src, k):
         def pair(j, acc):
-            y = 2 * j
-            left = jnp.concatenate([cz_ref[y], cz_ref[y + 1]], axis=1)
+            ys = [BATCH * j + u for u in range(BATCH)]
+            left = jnp.concatenate([cz_ref[y] for y in ys], axis=1)
             right = jnp.concatenate(
-                [
-                    src[pl.ds(y, 3), :, own : own + lanes].reshape(9 * CH, lanes),
-                    src[pl.ds(y + 1, 3), :, own : own + lanes].reshape(9 * CH, lanes),
-                ],
+                [src[pl.ds(y, 3), :, own : own + lanes].reshape(9 * CH, lanes) for y in ys],
                 axis=1,
             )
             return acc + lax.dot_general(
                 left, right, (((1,), (1,)), ((), ())), preferred_element_type=f32
             )
 
-        g_ref[k] = lax.fori_loop(0, cy // 2, pair, jnp.zeros((3 * CH, 9 * CH), f32))
+        g_ref[k] = lax.fori_loop(0, cy // BATCH, pair, jnp.zeros((3 * CH, 9 * CH), f32))
 
     weight_gradient(acts[LAYERS - 1], LAYERS - 1)
     source = cot_ref
@@ -269,16 +293,17 @@
         w = wb_ref[k]
         here = acts[k]
 
-        def backward(y, carry, w=w, here=here, source=source, k=k):
-            spread = convolve(source, w, y)
-            below = here[y + 1, CH : 2 * CH, :].astype(f32)
-            cot = spread * (1.0 - below * below)
-            if k > 1:
-                put(here, y, cot)
-            put_cz(y, cot)
+        def backward(j, carry, w=w, here=here, source=source, k=k):
+            ys = rows_at(j)
+            below = [here[y + 1, CH : 2 * CH, :].astype(f32) for y in ys]
+            cots = [v * (1.0 - b * b) for v, b in zip(convolve(source, w, ys), below)]
+            for y, cot in zip(ys, cots):
+                if k > 1:
+                    put(here, y, cot)
+                put_cz(y, cot)
             return carry
 
-        lax.fori_loop(0, cy, backward, 0)
+        lax.fori_loop(0, cy // unroll, backward, 0)
         weight_gradient(acts[k - 1], k - 1)
         source = here
 
@@ -329,7 +354,7 @@
 
 
 def stress_kernel(n, groups, zl, recv_ref, out_ref, fs_ref):
-    comps, cx, wide, depth = out_ref.shape
+    comps, cx, wide, _ = out_ref.shape
     srows = recv_ref.shape[1]
     lanes = recv_ref.shape[2]
     cz = n * zl
@@ -546,7 +571,6 @@
 
 def spread_table(n, cx, zl, fine_z):
     window = zl + 2
-    cz = fine_z // 2
     table = np.full((cx + 4, 1, 2 * fine_z), -1, np.int32)
     for k in range(cx + 4):
         for lane in range(2 * fine_z):
@@ -562,7 +586,7 @@
     return table
 
 
-def local(velocity, w_in, w_mid_a, w_mid_b, w_out):
+def step(velocity, w_in, w_mid_a, w_mid_b, w_out):
     n = lax.axis_size("slab")
     groups = lax.axis_size("grp")
     devices = n * groups
@@ -659,9 +683,7 @@
     )(*lower, mine, *upper, w_fwd, w_bwd, send_idx)
 
     st = lax.all_to_all(bsend, "slab", 0, 0, tiled=True)
-    partial_sums = lax.all_to_all(
-        grads.reshape(devices, per_device, 128), both, 0, 0, tiled=True
-    )
+    partial_sums = lax.all_to_all(grads.reshape(devices, per_device, 128), both, 0, 0, tiled=True)
     total = jnp.sum(partial_sums, axis=0)
     summed = lax.all_to_all(
         jnp.broadcast_to(total[None], (devices, per_device, 128)), both, 0, 0, tiled=True
@@ -706,4 +728,4 @@
 def solution(mesh):
     in_specs = (P(None, "slab", None, "grp"), P(), P(), P(), P())
     out_specs = (P(None, "slab", None, "grp"), P(None, "slab", "grp", None), P(), P(), P(), P())
-    return jax.shard_map(local, mesh=mesh, in_specs=in_specs, out_specs=out_specs, check_vma=False)
+    return jax.shard_map(step, mesh=mesh, in_specs=in_specs, out_specs=out_specs, check_vma=False)

time: 307 us -> 155 us (0.50)
  Pallas kernels: 214 us -> 59.6 us
  waiting for transfers between devices: 29.4 us -> 35.3 us
    pallas_call x6, Pallas kernels: 214 us -> 59.6 us  [the longest x1 40.1 us: step(): call(functools.partial(closure_kernel, (n, hops, groups, devices, cy, cx,...]
    ppermute x4, waiting for transfers between devices: 15.3 us -> 19.4 us  [shift(): return lax.ppermute(x, axis, [(i, (i + by) % count) for i in range(count)])]
    unnamed x46 -> x28, local copies, waits for them, and re-layouts: 11.4 us -> 9.15 us
  transfers between devices with their start and end apart: 9 -> 9, of which waited for: 6 -> 6; matrix products, arithmetic and copies ran while one was open for 3% -> 5% of each run, Pallas kernels for 3% -> 2%
where the time goes in v2:
time: 155 us; the launch traced here: 154 us
  Pallas kernels  59.6 us (38%)
  waiting for transfers between devices  35.3 us (23%)
  starting transfers between devices  25.3 us (16%)
  blocking collectives  21.5 us (14%)
  local copies, waits for them, and re-layouts  11.2 us (7%)
    pallas_call x1, Pallas kernels, step(): call(functools.partial(closure_kernel, (n, hops, groups, devices, cy, cx,...  40.1 us
    ppermute x4, waiting for transfers between devices, shift(): return lax.ppermute(x, axis, [(i, (i + by) % count) for i in range(count)])  19.4 us
    pallas_call x1, Pallas kernels, step(): call(functools.partial(advance_kernel, n), jax.ShapeDtypeStruct(velocity....  15.4 us
    all_to_all x1, blocking collectives, step(): lax.all_to_all(grads.reshape(devices, per_device, 128), both, 0, 0, tiled...  11.6 us
    all_to_all x1, blocking collectives, step(): lax.all_to_all(jnp.broadcast_to(total[None], (devices, per_device, 128)),...  9.88 us
    unnamed x28, local copies, waits for them, and re-layouts  9.15 us
    all_to_all x1, waiting for transfers between devices, step(): out_blocks = lax.all_to_all(ssend, both, 0, 0, tiled=True)  7.77 us
    ppermute x4, starting transfers between devices, shift(): return lax.ppermute(x, axis, [(i, (i + by) % count) for i in range(count)])  7.27 us
  transfers between devices with their start and end apart: 9, of which 6 were waited for; matrix products, arithmetic and copies ran while one was open for 5% of the time, Pallas kernels for 2%

profile of v2, /device:TPU:0, one launch (start us, length us, event | category | flops | bytes accessed | tf_op | source)
XLA Modules:
  0.0 153.9 jit_solution(16390659306121518992)
XLA Ops:
  0.6 0.0 copy-start
  0.6 1.2 copy-done
  1.8 0.4 shard_map.127
  2.2 0.5 collective-permute-start
  2.7 2.0 %collective-permute-start.1 = (bf16[144,128]{1,0:T(8,128)(2,1)S(1)}, bf16[144,128]{1,0:T(8,128)(2,1)S(1)}, u32[]{:S(2)}, u32[]{:S(2)}) collective-permute-start(bf16[144,128]{1,0:T(8,128)(2,1)S(1)} %get-tuple-element.19), channel_id=1, source_target_pairs={{0,24},{8,0},{16,8},{24,16},{1,25},{9,1},{17,9},{25,17},{2,26},{10... | collective-permute-start | bytes 110600 | tf_op jit(solution)/shard_map/ppermute | solution.py:608
  4.7 2.9 %shard_map.128 = bf16[8,96,128]{2,1,0:T(8,128)(2,1)} custom-call(f32[3,4,144,128]{3,2,1,0:T(8,128)S(1)} %copy-done), custom_call_target="tpu_custom_call" | custom-call | flops 4000000000 | bytes 10000000 | tf_op jit(solution)/shard_map/pallas_call | solution.py:624
  7.7 0.0 copy-start.6
  7.7 6.7 %all-to-all-start = ((bf16[8,96,128]{2,1,0:T(8,128)(2,1)}), bf16[8,96,128]{2,1,0:T(8,128)(2,1)S(1)}, u32[]{:S(2)}, u32[]{:S(2)}) async-start(bf16[8,96,128]{2,1,0:T(8,128)(2,1)} %shard_map.128), calls=%async_computation | async-start | bytes 393216 | tf_op jit(solution)/shard_map/all_to_all | solution.py:631
  14.3 0.0 copy-done.6
  14.3 0.0 copy-start.5
  14.4 0.2 copy.24
  14.6 0.5 copy-done.5
  15.1 0.1 copy.27
  15.3 0.0 copy-start.3
  15.3 0.8 copy-done.3
  16.1 0.0 copy-start.4
  16.1 0.2 copy.25
  16.3 0.6 copy-done.4
  16.9 0.2 copy.26
  17.1 0.0 copy-start.7
  17.2 0.0 copy-start.8
  17.2 0.1 pad_maximum_fusion
  17.3 0.5 copy-done.7
  17.8 0.0 copy-done.8
  17.9 4.5 %all-to-all-done.refs_1_ = bf16[8,96,128]{2,1,0:T(8,128)(2,1)S(1)} async-done(((bf16[8,96,128]{2,1,0:T(8,128)(2,1)}), bf16[8,96,128]{2,1,0:T(8,128)(2,1)S(1)}, u32[]{:S(2)}, u32[]{:S(2)}) %all-to-all-start) | async-done | bytes 196640 | tf_op jit(solution)/shard_map/all_to_all | solution.py:631
  22.3 1.0 collective-permute-start.2
  23.4 4.3 %collective-permute-start.3 = (bf16[8,96,128]{2,1,0:T(8,128)(2,1)S(1)}, bf16[8,96,128]{2,1,0:T(8,128)(2,1)S(1)}, u32[]{:S(2)}, u32[]{:S(2)}) collective-permute-start(bf16[8,96,128]{2,1,0:T(8,128)(2,1)S(1)} %all-to-all-done.refs_1_), channel_id=1, source_target_pairs={{0,31},{1,0},{2,1},{3,2},{4,3},{5,4},{6,5},{7,6},{8,7},{9,8},{10,9... | collective-permute-start | bytes 589832 | tf_op jit(solution)/shard_map/ppermute | solution.py:604
  27.7 0.5 copy.29
  28.2 0.3 reshape.35.refs_4_
  28.5 0.3 copy.28
  28.8 0.3 reshape.34.refs_3_
  29.1 0.0 collective-permute-done
  29.1 0.0 collective-permute-done.1
  29.1 1.9 %collective-permute-done.2.refs_0_ = bf16[8,96,128]{2,1,0:T(8,128)(2,1)S(1)} collective-permute-done((bf16[8,96,128]{2,1,0:T(8,128)(2,1)S(1)}, bf16[8,96,128]{2,1,0:T(8,128)(2,1)S(1)}, u32[]{:S(2)}, u32[]{:S(2)}) %collective-permute-start.2) | collective-permute-done | bytes 196640 | tf_op jit(solution)/shard_map/ppermute | solution.py:604
  31.0 1.7 %collective-permute-done.3.refs_2_ = bf16[8,96,128]{2,1,0:T(8,128)(2,1)S(1)} collective-permute-done((bf16[8,96,128]{2,1,0:T(8,128)(2,1)S(1)}, bf16[8,96,128]{2,1,0:T(8,128)(2,1)S(1)}, u32[]{:S(2)}, u32[]{:S(2)}) %collective-permute-start.3) | collective-permute-done | bytes 196640 | tf_op jit(solution)/shard_map/ppermute | solution.py:604
  32.8 40.1 %shard_map.129 = (bf16[8,216,128]{2,1,0:T(8,128)(2,1)}, bf16[32,16,128]{2,1,0:T(8,128)(2,1)}, f32[256,128]{1,0:T(8,128)S(1)}) custom-call(bf16[8,96,128]{2,1,0:T(8,128)(2,1)S(1)} %collective-permute-done.2.refs_0_, bf16[8,96,128]{2,1,0:T(8,128)(2,1)S(1)} %all-to-all-done.refs_1_, bf16[8,96,128]{2,1,0:T(8,128)(2,1)S(1)} %collective-permute-done.3.refs_2_, ...), custom_call_target="tpu_custom_call" | custom-call | flops 40000000000 | bytes 100000000 | tf_op jit(solution)/shard_map/pallas_call | solution.py:661
  72.9 11.6 %all_to_all.25 = f32[32,8,128]{2,1,0:T(8,128)S(1)} all-to-all(f32[32,8,128]{2,1,0:T(8,128)S(1)} %bitcast.11), channel_id=1, replica_groups=mesh['grp'=4,'slab'=8] {'grp','slab'}, dimensions={0} | all-to-all | bytes 262144 | tf_op jit(solution)/shard_map/all_to_all | solution.py:686
  84.5 2.6 %all-to-all-start.2 = ((bf16[32,16,128]{2,1,0:T(8,128)(2,1)}), bf16[32,16,128]{2,1,0:T(8,128)(2,1)S(1)}, u32[]{:S(2)}, u32[]{:S(2)}) async-start(bf16[32,16,128]{2,1,0:T(8,128)(2,1)} %get-tuple-element.26), calls=%async_computation.2 | async-start | bytes 262144 | tf_op jit(solution)/shard_map/all_to_all | solution.py:691
  87.1 7.8 %all-to-all-done.2.recv_ref = bf16[32,16,128]{2,1,0:T(8,128)(2,1)S(1)} async-done(((bf16[32,16,128]{2,1,0:T(8,128)(2,1)}), bf16[32,16,128]{2,1,0:T(8,128)(2,1)S(1)}, u32[]{:S(2)}, u32[]{:S(2)}) %all-to-all-start.2) | async-done | bytes 131104 | tf_op jit(solution)/shard_map/all_to_all | solution.py:691
  94.9 9.9 %all_to_all.26 = f32[32,8,128]{2,1,0:T(8,128)S(1)} all-to-all(f32[32,8,128]{2,1,0:T(8,128)S(1)} %broadcast_in_dim.2), channel_id=1, replica_groups=mesh['grp'=4,'slab'=8] {'grp','slab'}, dimensions={0} | all-to-all | bytes 262144 | tf_op jit(solution)/shard_map/all_to_all | solution.py:688
  104.8 3.5 %all-to-all-start.1 = ((bf16[8,216,128]{2,1,0:T(8,128)(2,1)}), bf16[8,216,128]{2,1,0:T(8,128)(2,1)S(1)}, u32[]{:S(2)}, u32[]{:S(2)}) async-start(bf16[8,216,128]{2,1,0:T(8,128)(2,1)} %get-tuple-element.25), calls=%async_computation.1 | async-start | bytes 884736 | tf_op jit(solution)/shard_map/all_to_all | solution.py:685
  108.2 0.8 constant_dynamic-update-slice_fusion.1
  109.0 0.6 constant_dynamic-update-slice_fusion
  109.7 1.9 %collective-permute-start.4 = (bf16[2016,128]{1,0:T(8,128)(2,1)}, bf16[2016,128]{1,0:T(8,128)(2,1)S(1)}, u32[]{:S(2)}, u32[]{:S(2)}) collective-permute-start(bf16[2016,128]{1,0:T(8,128)(2,1)} %constant_dynamic-update-slice_fusion), channel_id=1, source_target_pairs={{0,1},{1,2},{2,3},{3,4},{4,5},{5,6},{6,7},{7,0},{8,9},{9,10},{10,1... | collective-permute-start | bytes 1548296 | tf_op jit(solution)/shard_map/ppermute | solution.py:608
  111.6 2.8 %collective-permute-start.5 = (bf16[2016,128]{1,0:T(8,128)(2,1)}, bf16[2016,128]{1,0:T(8,128)(2,1)S(1)}, u32[]{:S(2)}, u32[]{:S(2)}) collective-permute-start(bf16[2016,128]{1,0:T(8,128)(2,1)} %constant_dynamic-update-slice_fusion), channel_id=1, source_target_pairs={{0,7},{1,0},{2,1},{3,2},{4,3},{5,4},{6,5},{7,6},{8,15},{9,8},{10,9... | collective-permute-start | bytes 1548296 | tf_op jit(solution)/shard_map/ppermute | solution.py:608
  114.4 0.4 shard_map.131
  114.8 0.7 copy.30
  115.6 0.3 shard_map.132
  115.8 0.0 copy-start.1
  115.8 0.8 copy.32
  116.7 0.8 copy.33
  117.5 0.7 copy.34
  118.2 0.0 copy-start.2
  118.2 0.8 copy.31
  119.0 17.4 %collective-permute-done.4.xl_ref = bf16[2016,128]{1,0:T(8,128)(2,1)S(1)} collective-permute-done((bf16[2016,128]{1,0:T(8,128)(2,1)}, bf16[2016,128]{1,0:T(8,128)(2,1)S(1)}, u32[]{:S(2)}, u32[]{:S(2)}) %collective-permute-start.4) | collective-permute-done | bytes 516128 | tf_op jit(solution)/shard_map/ppermute | solution.py:608
  136.4 2.0 %collective-permute-done.5.xr_ref = bf16[2016,128]{1,0:T(8,128)(2,1)S(1)} collective-permute-done((bf16[2016,128]{1,0:T(8,128)(2,1)}, bf16[2016,128]{1,0:T(8,128)(2,1)S(1)}, u32[]{:S(2)}, u32[]{:S(2)}) %collective-permute-start.5) | collective-permute-done | bytes 516128 | tf_op jit(solution)/shard_map/ppermute | solution.py:608
  138.5 0.0 all-to-all-done.1.st_ref
  138.5 0.0 copy-done.1
  138.5 0.0 copy-done.2
  138.5 15.4 %shard_map.130 = f32[3,4,144,128]{3,2,1,0:T(8,128)} custom-call(f32[3,4,144,128]{3,2,1,0:T(8,128)S(1)} %copy-done.1, bf16[288,128]{1,0:T(8,128)(2,1)S(1)} %pad_maximum_fusion.1.ez_ref, bf16[2016,128]{1,0:T(8,128)(2,1)S(1)} %collective-permute-done.4.xl_ref, bf16[2016,128]{1,0:T(8,128)(2,1)S(1)} %collective-permute-done.5.xr_ref, ...), custom_call_target="tpu_custom_call" | custom-call | flops 15000000512 | bytes 37500000 | tf_op jit(solution)/shard_map/pallas_call | solution.py:693
  (7 shorter events, 0.2 us)
Async XLA Ops:
  0.6 1.2 copy-start
  2.2 26.9 %collective-permute-start = (bf16[144,128]{1,0:T(8,128)(2,1)S(1)}, bf16[144,128]{1,0:T(8,128)(2,1)S(1)}, u32[]{:S(2)}, u32[]{:S(2)}) collective-permute-start(bf16[144,128]{1,0:T(8,128)(2,1)S(1)} %get-tuple-element.19), channel_id=1, source_target_pairs={{0,8},{8,16},{16,24},{24,0},{1,9},{9,17},{17,25},{25,1},{2,10},{10... | collective-permute-start | bytes 110600 | tf_op jit(solution)/shard_map/ppermute | solution.py:608
  2.7 26.4 %collective-permute-start.1 = (bf16[144,128]{1,0:T(8,128)(2,1)S(1)}, bf16[144,128]{1,0:T(8,128)(2,1)S(1)}, u32[]{:S(2)}, u32[]{:S(2)}) collective-permute-start(bf16[144,128]{1,0:T(8,128)(2,1)S(1)} %get-tuple-element.19), channel_id=1, source_target_pairs={{0,24},{8,0},{16,8},{24,16},{1,25},{9,1},{17,9},{25,17},{2,26},{10... | collective-permute-start | bytes 110600 | tf_op jit(solution)/shard_map/ppermute | solution.py:608
  7.7 6.7 %copy-start.6 = (bf16[27,16,3]{0,1,2:T(8,128)(2,1)S(1)}, bf16[27,16,3]{0,1,2:T(8,128)(2,1)}, u32[]{:S(2)}) copy-start(bf16[27,16,3]{0,1,2:T(8,128)(2,1)} %param.9) | copy-start | bytes 7780
  7.7 14.7 %all-to-all-start = ((bf16[8,96,128]{2,1,0:T(8,128)(2,1)}), bf16[8,96,128]{2,1,0:T(8,128)(2,1)S(1)}, u32[]{:S(2)}, u32[]{:S(2)}) async-start(bf16[8,96,128]{2,1,0:T(8,128)(2,1)} %shard_map.128), calls=%async_computation | async-start | bytes 393216 | tf_op jit(solution)/shard_map/all_to_all | solution.py:631
  14.3 0.7 copy-start.5
  15.3 0.8 copy-start.3
  16.1 0.8 copy-start.4
  17.1 0.7 copy-start.7
  17.2 0.7 copy-start.8
  22.3 8.7 %collective-permute-start.2 = (bf16[8,96,128]{2,1,0:T(8,128)(2,1)S(1)}, bf16[8,96,128]{2,1,0:T(8,128)(2,1)S(1)}, u32[]{:S(2)}, u32[]{:S(2)}) collective-permute-start(bf16[8,96,128]{2,1,0:T(8,128)(2,1)S(1)} %all-to-all-done.refs_1_), channel_id=1, source_target_pairs={{0,1},{1,2},{2,3},{3,4},{4,5},{5,6},{6,7},{7,8},{8,9},{9,10},{10,1... | collective-permute-start | bytes 589832 | tf_op jit(solution)/shard_map/ppermute | solution.py:604
  23.4 9.4 %collective-permute-start.3 = (bf16[8,96,128]{2,1,0:T(8,128)(2,1)S(1)}, bf16[8,96,128]{2,1,0:T(8,128)(2,1)S(1)}, u32[]{:S(2)}, u32[]{:S(2)}) collective-permute-start(bf16[8,96,128]{2,1,0:T(8,128)(2,1)S(1)} %all-to-all-done.refs_1_), channel_id=1, source_target_pairs={{0,31},{1,0},{2,1},{3,2},{4,3},{5,4},{6,5},{7,6},{8,7},{9,8},{10,9... | collective-permute-start | bytes 589832 | tf_op jit(solution)/shard_map/ppermute | solution.py:604
  84.5 10.4 %all-to-all-start.2 = ((bf16[32,16,128]{2,1,0:T(8,128)(2,1)}), bf16[32,16,128]{2,1,0:T(8,128)(2,1)S(1)}, u32[]{:S(2)}, u32[]{:S(2)}) async-start(bf16[32,16,128]{2,1,0:T(8,128)(2,1)} %get-tuple-element.26), calls=%async_computation.2 | async-start | bytes 262144 | tf_op jit(solution)/shard_map/all_to_all | solution.py:691
  104.8 33.7 %all-to-all-start.1 = ((bf16[8,216,128]{2,1,0:T(8,128)(2,1)}), bf16[8,216,128]{2,1,0:T(8,128)(2,1)S(1)}, u32[]{:S(2)}, u32[]{:S(2)}) async-start(bf16[8,216,128]{2,1,0:T(8,128)(2,1)} %get-tuple-element.25), calls=%async_computation.1 | async-start | bytes 884736 | tf_op jit(solution)/shard_map/all_to_all | solution.py:685
  109.7 26.7 %collective-permute-start.4 = (bf16[2016,128]{1,0:T(8,128)(2,1)}, bf16[2016,128]{1,0:T(8,128)(2,1)S(1)}, u32[]{:S(2)}, u32[]{:S(2)}) collective-permute-start(bf16[2016,128]{1,0:T(8,128)(2,1)} %constant_dynamic-update-slice_fusion), channel_id=1, source_target_pairs={{0,1},{1,2},{2,3},{3,4},{4,5},{5,6},{6,7},{7,0},{8,9},{9,10},{10,1... | collective-permute-start | bytes 1548296 | tf_op jit(solution)/shard_map/ppermute | solution.py:608
  111.6 26.9 %collective-permute-start.5 = (bf16[2016,128]{1,0:T(8,128)(2,1)}, bf16[2016,128]{1,0:T(8,128)(2,1)S(1)}, u32[]{:S(2)}, u32[]{:S(2)}) collective-permute-start(bf16[2016,128]{1,0:T(8,128)(2,1)} %constant_dynamic-update-slice_fusion), channel_id=1, source_target_pairs={{0,7},{1,0},{2,1},{3,2},{4,3},{5,4},{6,5},{7,6},{8,15},{9,8},{10,9... | collective-permute-start | bytes 1548296 | tf_op jit(solution)/shard_map/ppermute | solution.py:608
  115.8 22.6 %copy-start.1 = (f32[3,4,144,128]{3,2,1,0:T(8,128)S(1)}, f32[3,4,144,128]{3,2,1,0:T(8,128)}, u32[]{:S(2)}) copy-start(f32[3,4,144,128]{3,2,1,0:T(8,128)} %v_ref.5) | copy-start | bytes 2654212
  118.2 20.2 %copy-start.2 = (s32[6,1,256]{2,1,0:T(1,128)S(1)}, s32[6,1,256]{2,1,0:T(1,128)}, u32[]{:S(2)}) copy-start(s32[6,1,256]{2,1,0:T(1,128)} %constant.19.clone.idx_ref) | copy-start | bytes 18436

commit v3 on v2

--- a/solution.py
+++ b/solution.py
@@ -15,6 +15,7 @@
 stress_pairs = ((0, 0), (1, 1), (2, 2), (0, 1), (0, 2), (1, 2))
 LAYERS = 4
 CH = 16
+SPAN = 3
 MARGIN = LAYERS + LAYERS - 1
 f32 = jnp.float32
 bf16 = jnp.bfloat16
@@ -32,18 +33,23 @@
 
 
 def nbytes(shapes):
-    return sum(int(np.prod(x.shape)) * jnp.dtype(x.dtype).itemsize for x in shapes)
-
-
-def call(body, out_shape, scratch, cost, n_in):
+    return sum(
+        int(np.prod(x.shape)) * jnp.dtype(x.dtype).itemsize
+        for x in shapes
+        if hasattr(x, "memory_space") and x.memory_space == pltpu.VMEM
+    )
+
+
+def call(body, out_shape, scratch, cost, n_in, low=36, far_in=0, far_out=0):
     many = isinstance(out_shape, (tuple, list))
-    grant = max(36 * MIB, min(62 * MIB, int(1.1 * nbytes(scratch)) + 9 * MIB))
+    grant = max(low * MIB, min(62 * MIB, int(1.1 * nbytes(scratch)) + 9 * MIB))
     spec = pl.BlockSpec(memory_space=pltpu.VMEM)
+    far = pl.BlockSpec(memory_space=pltpu.HBM)
     return pl.pallas_call(
         body,
         out_shape=out_shape,
-        in_specs=[spec] * n_in,
-        out_specs=[spec] * len(out_shape) if many else spec,
+        in_specs=[spec] * (n_in - far_in) + [far] * far_in,
+        out_specs=[spec] * (len(out_shape) - far_out) + [far] * far_out if many else spec,
         scratch_shapes=scratch,
         compiler_params=pltpu.CompilerParams(vmem_limit_bytes=grant),
         cost_estimate=pl.CostEstimate(flops=cost, bytes_accessed=cost // 400, transcendentals=0),
@@ -146,18 +152,7 @@
     e_ref[...] = total.astype(bf16)
 
 
-def closure_kernel(dims, *refs):
-    n, hops, groups, _, cy, _, zl, length = dims
-    nt = 2 * hops + 1
-    tiles = refs[:nt]
-    wf_ref, wb_ref, idx_ref = refs[nt : nt + 3]
-    bsend_ref, ssend_ref, grad_ref = refs[nt + 3 : nt + 6]
-    acts = refs[nt + 6 : nt + 10]
-    cot_ref, cz_ref, f_ref, fs_ref, g_ref = refs[nt + 10 :]
-    unroll = max(u for u in range(1, cy + 1) if cy % u == 0 and u * nt <= 36)
-    group = tiles[0].shape[1]
-    lanes = tiles[0].shape[2]
-    own = hops * lanes
+def closure_tools(nt, hops, lanes, zl, unroll):
     zpos = lax.broadcasted_iota(jnp.int32, (CH, lanes), 1) & (zl - 1)
     first_z = zpos == 0
     last_z = zpos == zl - 1
@@ -186,29 +181,64 @@
             ref[y + 1, CH : 2 * CH, at] = v.astype(bf16)
             ref[y + 1, 2 * CH : 3 * CH, at] = pltpu.roll(v, lanes - zl, 1).astype(bf16)
 
-    def put_cz(y, value):
+    def put_cz(cz_ref, y, value):
         value = rounded(value)
         cz_ref[y, 0:CH, :] = after(value, hops).astype(bf16)
         cz_ref[y, CH : 2 * CH, :] = tile(value, hops).astype(bf16)
         cz_ref[y, 2 * CH : 3 * CH, :] = before(value, hops).astype(bf16)
 
     def convolve(src, w, ys):
-        results = []
-        for y in ys:
-            columns = src[pl.ds(y, 3)].reshape(9 * CH, nt * lanes)
-            results.append(jnp.dot(w, columns, preferred_element_type=f32))
         sums = []
-        for parts in results:
-            low, mid, high = parts[0:CH], parts[CH : 2 * CH], parts[2 * CH :]
-            sums.append(
-                jnp.concatenate(
-                    [tile(mid, t) + before(low, t) + after(high, t) for t in range(nt)], axis=1
+        for first in range(0, len(ys), 2 * SPAN):
+            columns = jnp.concatenate(
+                [
+                    src[pl.ds(ys[at], SPAN + 2)].reshape((SPAN + 2) * 3 * CH, nt * lanes)
+                    for at in range(first, first + 2 * SPAN, SPAN)
+                ],
+                axis=1,
+            )
+            results = jnp.dot(w, columns, preferred_element_type=f32)
+            for u in range(2 * SPAN):
+                at = (u // SPAN) * nt * lanes
+                parts = results[
+                    (u % SPAN) * 3 * CH : (u % SPAN + 1) * 3 * CH, at : at + nt * lanes
+                ]
+                low, mid, high = parts[0:CH], parts[CH : 2 * CH], parts[2 * CH :]
+                sums.append(
+                    jnp.concatenate(
+                        [tile(mid, t) + before(low, t) + after(high, t) for t in range(nt)], axis=1
+                    )
                 )
-            )
         return sums
 
     def rows_at(j):
         return [unroll * j + u for u in range(unroll)]
+
+    return tile, put, put_cz, convolve, rows_at
+
+
+def stored(far_ref, i, near_ref):
+    rows, _, columns = near_ref.shape
+    return far_ref.at[i, 0:rows, :, 0:columns]
+
+
+def forward_kernel(dims, *refs):
+    n, hops, groups, _, cy, _, zl, length, unroll = dims
+    nt = 2 * hops + 1
+    tiles = refs[:nt]
+    wf_ref, idx_ref = refs[nt : nt + 2]
+    bsend_ref, ssend_ref = refs[nt + 2 : nt + 4]
+    far_ref = refs[nt + 4]
+    acts = refs[nt + 5 : nt + 9]
+    cot_ref, cz_ref, f_ref, fs_ref, sems = refs[nt + 9 :]
+    near = (*acts, cot_ref, cz_ref)
+
+    def save(i):
+        return pltpu.make_async_copy(near[i], stored(far_ref, i, near[i]), sems.at[i])
+
+    group = tiles[0].shape[1]
+    lanes = tiles[0].shape[2]
+    tile, put, put_cz, convolve, rows_at = closure_tools(nt, hops, lanes, zl, unroll)
 
     for ref in (*acts, cot_ref):
         zero = jnp.zeros((3 * CH, nt * lanes), bf16)
@@ -237,6 +267,7 @@
         return carry
 
     lax.fori_loop(0, cy // unroll, start, 0)
+    save(0).start()
 
     for k in range(LAYERS - 1):
         w = wf_ref[k]
@@ -249,6 +280,7 @@
             return carry
 
         lax.fori_loop(0, cy // unroll, forward, 0)
+        save(k + 1).start()
 
     w_last = wf_ref[LAYERS - 1]
     channel = lax.broadcasted_iota(jnp.int32, (CH, nt * lanes), 0)
@@ -264,7 +296,7 @@
         ]
         for y, cot in zip(ys, cots):
             put(cot_ref, y, cot)
-            put_cz(y, cot)
+            put_cz(cz_ref, y, cot)
         for y, v in zip(ys, predicted):
             stress = rounded(v)
             for t in range(nt):
@@ -272,8 +304,60 @@
         return carry
 
     lax.fori_loop(0, cy // unroll, predict, 0)
-
-    def weight_gradient(src, k):
+    save(LAYERS).start()
+    save(LAYERS + 1).start()
+
+    left = jnp.concatenate(
+        [
+            f_ref[t, (3 + 3 * half) * cy : (6 + 3 * half) * cy, :].astype(bf16)
+            for half in range(2)
+            for t in range(nt)
+        ],
+        axis=1,
+    )
+    row = lax.broadcasted_iota(jnp.int32, (2 * nt * lanes, 256), 0)
+    for d in range(n // 2):
+        pick = jnp.where(row == idx_ref[d], 1.0, 0.0).astype(bf16)
+        moved = jnp.dot(left, pick, preferred_element_type=f32).astype(bf16)
+        bsend_ref[2 * d] = moved[:, 0:128]
+        bsend_ref[2 * d + 1] = moved[:, 128:256]
+
+    wide = cy // groups
+    srows = ssend_ref.shape[1]
+    fs_ref[...] = jnp.zeros(fs_ref.shape, f32)
+    for g in range(groups):
+        for c in range(6):
+            at = (3 + c) * cy + g * wide
+            fs_ref[c * wide : (c + 1) * wide, :] = f_ref[hops, at : at + wide, :]
+        for j in range(srows // 16):
+            parts = granule_swap(
+                [fs_ref[r * srows + 16 * j : r * srows + 16 * j + 16, :] for r in range(n)]
+            )
+            for d in range(n):
+                ssend_ref[g * n + d, 16 * j : 16 * j + 16, :] = parts[d]
+    for i in range(LAYERS + 2):
+        save(i).wait()
+
+
+def backward_kernel(dims, *refs):
+    _, hops, _, devices, cy, _, zl, _, unroll = dims
+    nt = 2 * hops + 1
+    wb_ref, ssend_ref = refs[:2]
+    far_ref, sum_ref = refs[2:4]
+    acts = refs[4:8]
+    cot_ref, cz_in_ref, cz_ref, g_ref, grad_ref, sems = refs[8:]
+    near = (*acts, cot_ref, cz_in_ref)
+
+    def fetch(i):
+        return pltpu.make_async_copy(stored(far_ref, i, near[i]), near[i], sems.at[i])
+
+    for i in (LAYERS + 1, LAYERS - 1, LAYERS, *range(LAYERS - 2, -1, -1)):
+        fetch(i).start()
+    lanes = ssend_ref.shape[2]
+    own = hops * lanes
+    _, put, put_cz, convolve, rows_at = closure_tools(nt, hops, lanes, zl, unroll)
+
+    def weight_gradient(src, cz_ref, k):
         def pair(j, acc):
             ys = [BATCH * j + u for u in range(BATCH)]
             left = jnp.concatenate([cz_ref[y] for y in ys], axis=1)
@@ -287,7 +371,10 @@
 
         g_ref[k] = lax.fori_loop(0, cy // BATCH, pair, jnp.zeros((3 * CH, 9 * CH), f32))
 
-    weight_gradient(acts[LAYERS - 1], LAYERS - 1)
+    fetch(LAYERS + 1).wait()
+    fetch(LAYERS - 1).wait()
+    weight_gradient(acts[LAYERS - 1], cz_in_ref, LAYERS - 1)
+    fetch(LAYERS).wait()
     source = cot_ref
     for k in range(LAYERS - 1, 0, -1):
         w = wb_ref[k]
@@ -300,11 +387,12 @@
             for y, cot in zip(ys, cots):
                 if k > 1:
                     put(here, y, cot)
-                put_cz(y, cot)
+                put_cz(cz_ref, y, cot)
             return carry
 
         lax.fori_loop(0, cy // unroll, backward, 0)
-        weight_gradient(acts[k - 1], k - 1)
+        fetch(k - 1).wait()
+        weight_gradient(acts[k - 1], cz_ref, k - 1)
         source = here
 
     rows = LAYERS * 3 * CH
@@ -323,45 +411,25 @@
             (grad_ref.shape[0] - rows - rows // 8, main), f32
         )
 
-    left = jnp.concatenate(
-        [
-            f_ref[t, (3 + 3 * half) * cy : (6 + 3 * half) * cy, :].astype(bf16)
-            for half in range(2)
-            for t in range(nt)
-        ],
-        axis=1,
-    )
-    row = lax.broadcasted_iota(jnp.int32, (2 * nt * lanes, 256), 0)
-    for d in range(n // 2):
-        pick = jnp.where(row == idx_ref[d], 1.0, 0.0).astype(bf16)
-        moved = jnp.dot(left, pick, preferred_element_type=f32).astype(bf16)
-        bsend_ref[2 * d] = moved[:, 0:128]
-        bsend_ref[2 * d + 1] = moved[:, 128:256]
-
-    wide = cy // groups
-    srows = ssend_ref.shape[1]
-    fs_ref[...] = jnp.zeros(fs_ref.shape, f32)
-    for g in range(groups):
-        for c in range(6):
-            at = (3 + c) * cy + g * wide
-            fs_ref[c * wide : (c + 1) * wide, :] = f_ref[hops, at : at + wide, :]
-        for j in range(srows // 16):
-            parts = granule_swap(
-                [fs_ref[r * srows + 16 * j : r * srows + 16 * j + 16, :] for r in range(n)]
-            )
-            for d in range(n):
-                ssend_ref[g * n + d, 16 * j : 16 * j + 16, :] = parts[d].astype(bf16)
+    share = grad_ref.shape[0] // devices
+    for d in range(devices):
+        sum_ref[d, 0:share, :] = grad_ref[d * share : (d + 1) * share, :]
+        sum_ref[d, share:, :] = ssend_ref[d]
 
 
 def stress_kernel(n, groups, zl, recv_ref, out_ref, fs_ref):
     comps, cx, wide, _ = out_ref.shape
-    srows = recv_ref.shape[1]
+    srows = fs_ref.shape[1] // n
+    skip = recv_ref.shape[1] - srows
     lanes = recv_ref.shape[2]
     cz = n * zl
     for g in range(groups):
         for j in range(srows // 16):
             parts = granule_swap(
-                [recv_ref[g * n + s, 16 * j : 16 * j + 16, :].astype(f32) for s in range(n)]
+                [
+                    recv_ref[g * n + s, skip + 16 * j : skip + 16 * j + 16, :]
+                    for s in range(n)
+                ]
             )
             for r in range(n):
                 fs_ref[g, r * srows + 16 * j : r * srows + 16 * j + 16, :] = parts[r]
@@ -620,6 +688,17 @@
         LAYERS, 3 * CH, 9 * CH
     )
 
+    w_fwd, w_bwd = (
+        jnp.concatenate(
+            [
+                jnp.pad(w, ((0, 0), (0, 0), (3 * CH * u, 3 * CH * (SPAN - 1 - u))))
+                for u in range(SPAN)
+            ],
+            axis=1,
+        )
+        for w in (w_fwd, w_bwd)
+    )
+
     group = round_up(-(-9 * cy // n), 16)
     fields = call(
         functools.partial(filter_kernel, n),
@@ -658,38 +737,54 @@
     grad_rows = LAYERS * 3 * CH * 9 // 8
     per_device = round_up(-(-grad_rows // devices), 8)
     act = pltpu.VMEM((cy + 2, 3 * CH, nt * lanes), bf16)
-    bsend, ssend, grads = call(
-        functools.partial(
-            closure_kernel, (n, hops, groups, devices, cy, cx, zl, length)
-        ),
+    unroll = max(
+        u for u in range(1, cy + 1) if cy % u == 0 and u % (2 * SPAN) == 0 and u * nt <= 54
+    )
+    dims = (n, hops, groups, devices, cy, cx, zl, length, unroll)
+    act = ((cy + 2, 3 * CH, nt * lanes), bf16)
+    cz_shape = ((cy, 3 * CH, lanes), bf16)
+    bsend, ssend, saved = call(
+        functools.partial(forward_kernel, dims),
         (
             jax.ShapeDtypeStruct((n, 3 * cy, 128), bf16),
-            jax.ShapeDtypeStruct((devices, srows, lanes), bf16),
-            jax.ShapeDtypeStruct((devices * per_device, 128), f32),
+            jax.ShapeDtypeStruct((devices, srows, lanes), f32),
+            jax.ShapeDtypeStruct((LAYERS + 2, *act[0]), bf16),
         ),
         [
-            act,
-            act,
-            act,
-            act,
-            act,
-            pltpu.VMEM((cy, 3 * CH, lanes), bf16),
+            *[pltpu.VMEM(*act)] * (LAYERS + 1),
+            pltpu.VMEM(*cz_shape),
             pltpu.VMEM((nt, max(CH * cy, n * group), lanes), f32),
             pltpu.VMEM((n * srows, lanes), f32),
+            pltpu.SemaphoreType.DMA((LAYERS + 2,)),
+        ],
+        20_000_000_000,
+        nt + 2,
+        low=52,
+        far_out=1,
+    )(*lower, mine, *upper, w_fwd, send_idx)
+    to_sum = call(
+        functools.partial(backward_kernel, dims),
+        jax.ShapeDtypeStruct((devices, per_device + srows, lanes), f32),
+        [
+            *[pltpu.VMEM(*act)] * (LAYERS + 1),
+            pltpu.VMEM(*cz_shape),
+            pltpu.VMEM(*cz_shape),
             pltpu.VMEM((LAYERS, 3 * CH, 9 * CH), f32),
+            pltpu.VMEM((devices * per_device, lanes), f32),
+            pltpu.SemaphoreType.DMA((LAYERS + 2,)),
         ],
-        40_000_000_000,
-        nt + 3,
-    )(*lower, mine, *upper, w_fwd, w_bwd, send_idx)
+        20_000_000_000,
+        3,
+        low=52,
+        far_in=1,
+    )(w_bwd, ssend, saved)
 
     st = lax.all_to_all(bsend, "slab", 0, 0, tiled=True)
-    partial_sums = lax.all_to_all(grads.reshape(devices, per_device, 128), both, 0, 0, tiled=True)
-    total = jnp.sum(partial_sums, axis=0)
+    arrived = lax.all_to_all(to_sum, both, 0, 0, tiled=True)
+    total = jnp.sum(arrived[:, :per_device], axis=0)
     summed = lax.all_to_all(
         jnp.broadcast_to(total[None], (devices, per_device, 128)), both, 0, 0, tiled=True
     ).reshape(devices * per_device, 128)
-    out_blocks = lax.all_to_all(ssend, both, 0, 0, tiled=True)
-
     velocity_next = call(
         functools.partial(advance_kernel, n),
         jax.ShapeDtypeStruct(velocity.shape, f32),
@@ -709,7 +804,7 @@
         [pltpu.VMEM((groups, n * srows, lanes), f32)],
         1_000_000_000,
         1,
-    )(out_blocks)
+    )(arrived)
     grad_in, grad_mid_a, grad_mid_b, grad_out = call(
         unpack_kernel,
         (

time: 155 us -> 143 us (0.923)
  waiting for transfers between devices: 35.3 us -> 26.1 us
  blocking collectives: 21.5 us -> 15.1 us
  starting transfers between devices: 25.3 us -> 31.3 us
  local copies, waits for them, and re-layouts: 11.2 us -> 9.42 us
    ppermute x4, waiting for transfers between devices: 19.4 us -> 2.75 us  [shift(): return lax.ppermute(x, axis, [(i, (i + by) % count) for i in range(count)])]
    all_to_all x1, starting transfers between devices: 2.58 us -> 12.5 us  [step(): lax.all_to_all(jnp.broadcast_to(total[None], (devices, per_device, 128)),...]
    all_to_all x1, waiting for transfers between devices: 7.77 us -> 0.01 us  [step(): lax.all_to_all(jnp.broadcast_to(total[None], (devices, per_device, 128)),...]
    all_to_all x1, waiting for transfers between devices: 0.01 us -> 6.79 us  [step(): st = lax.all_to_all(bsend, 'slab', 0, 0, tiled=True)]
    ppermute x2, waiting for transfers between devices: 3.65 us -> 10.3 us  [ring(): lax.ppermute(x, both, [(i, (i + shift) % devices) for i in range(devices)])]
    all_to_all x2 -> x1, blocking collectives: 21.5 us -> 15.1 us  [step(): arrived = lax.all_to_all(to_sum, both, 0, 0, tiled=True)]
    ppermute x2, starting transfers between devices: 5.34 us -> 2.41 us  [ring(): lax.ppermute(x, both, [(i, (i + shift) % devices) for i in range(devices)])]
    unnamed x28, local copies, waits for them, and re-layouts: 9.15 us -> 6.69 us
  transfers between devices with their start and end apart: 9 -> 9, of which waited for: 6 -> 5; matrix products, arithmetic and copies ran while one was open for 5% -> 4% of each run, Pallas kernels for 2% -> 13%
where the time goes in v3:
time: 143 us
  Pallas kernels  59.3 us (41%)
  starting transfers between devices  31.3 us (22%)
  waiting for transfers between devices  26.1 us (18%)
  blocking collectives  15.1 us (11%)
  local copies, waits for them, and re-layouts  9.42 us (7%)
    pallas_call x1, Pallas kernels, step(): call(functools.partial(forward_kernel, dims), (jax.ShapeDtypeStruct((n, 3...  20.3 us
    pallas_call x1, Pallas kernels, step(): call(functools.partial(backward_kernel, dims), jax.ShapeDtypeStruct((devi...  19.5 us
    pallas_call x1, Pallas kernels, step(): call(functools.partial(advance_kernel, n), jax.ShapeDtypeStruct(velocity....  15.4 us
    all_to_all x1, blocking collectives, step(): arrived = lax.all_to_all(to_sum, both, 0, 0, tiled=True)  15.1 us
    all_to_all x1, starting transfers between devices, step(): lax.all_to_all(jnp.broadcast_to(total[None], (devices, per_device, 128)),...  12.5 us
    ppermute x2, waiting for transfers between devices, ring(): lax.ppermute(x, both, [(i, (i + shift) % devices) for i in range(devices)])  10.3 us
    ppermute x4, starting transfers between devices, shift(): return lax.ppermute(x, axis, [(i, (i + by) % count) for i in range(count)])  7.15 us
    all_to_all x1, waiting for transfers between devices, step(): st = lax.all_to_all(bsend, 'slab', 0, 0, tiled=True)  6.79 us
  transfers between devices with their start and end apart: 9, of which 5 were waited for; matrix products, arithmetic and copies ran while one was open for 4% of the time, Pallas kernels for 13%

profile of v3, /device:TPU:0, one launch (start us, length us, event | category | flops | bytes accessed | tf_op | source)
XLA Modules:
  0.0 142.6 jit_solution(4359850878276712077)
XLA Ops:
  0.6 0.0 copy-start
  0.6 1.2 copy-done
  1.8 0.0 copy-start.5
  1.8 0.0 copy-start.6
  1.8 0.0 copy-start.3
  1.8 0.0 copy-start.4
  1.8 0.0 copy-start.7
  1.8 0.0 copy-start.8
  1.8 0.4 shard_map.127
  2.2 2.5 %collective-permute-start.1 = (bf16[144,128]{1,0:T(8,128)(2,1)S(1)}, bf16[144,128]{1,0:T(8,128)(2,1)S(1)}, u32[]{:S(2)}, u32[]{:S(2)}) collective-permute-start(bf16[144,128]{1,0:T(8,128)(2,1)S(1)} %get-tuple-element.19), channel_id=1, source_target_pairs={{0,24},{8,0},{16,8},{24,16},{1,25},{9,1},{17,9},{25,17},{2,26},{10... | collective-permute-start | bytes 110600 | tf_op jit(solution)/shard_map/ppermute | solution.py:676
  4.7 0.0 collective-permute-start
  4.7 2.9 %shard_map.128 = bf16[8,96,128]{2,1,0:T(8,128)(2,1)} custom-call(f32[3,4,144,128]{3,2,1,0:T(8,128)S(1)} %copy-done), custom_call_target="tpu_custom_call" | custom-call | flops 4000000000 | bytes 10000000 | tf_op jit(solution)/shard_map/pallas_call | solution.py:703
  7.7 5.8 %all-to-all-start = ((bf16[8,96,128]{2,1,0:T(8,128)(2,1)}), bf16[8,96,128]{2,1,0:T(8,128)(2,1)S(1)}, u32[]{:S(2)}, u32[]{:S(2)}) async-start(bf16[8,96,128]{2,1,0:T(8,128)(2,1)} %shard_map.128), calls=%async_computation | async-start | bytes 393216 | tf_op jit(solution)/shard_map/all_to_all | solution.py:710
  13.5 0.0 copy-done.5
  13.5 0.1 copy.27
  13.6 0.0 copy-done.6
  13.6 0.2 copy.24
  13.9 0.0 copy-done.3
  13.9 0.2 copy.25
  14.1 0.0 copy-done.4
  14.2 0.2 copy.26
  14.3 0.1 pad_maximum_fusion
  14.5 0.5 copy.29
  15.0 0.3 reshape.32
  15.3 0.3 copy.28
  15.6 0.3 reshape.31
  15.9 0.1 fusion.10.refs_0_
  16.0 0.0 copy-done.7
  16.0 0.0 copy-done.8
  16.1 6.3 %all-to-all-done.refs_1_ = bf16[8,96,128]{2,1,0:T(8,128)(2,1)S(1)} async-done(((bf16[8,96,128]{2,1,0:T(8,128)(2,1)}), bf16[8,96,128]{2,1,0:T(8,128)(2,1)S(1)}, u32[]{:S(2)}, u32[]{:S(2)}) %all-to-all-start) | async-done | bytes 196640 | tf_op jit(solution)/shard_map/all_to_all | solution.py:710
  22.3 2.4 %collective-permute-start.3 = (bf16[8,96,128]{2,1,0:T(8,128)(2,1)S(1)}, bf16[8,96,128]{2,1,0:T(8,128)(2,1)S(1)}, u32[]{:S(2)}, u32[]{:S(2)}) collective-permute-start(bf16[8,96,128]{2,1,0:T(8,128)(2,1)S(1)} %all-to-all-done.refs_1_), channel_id=1, source_target_pairs={{0,31},{1,0},{2,1},{3,2},{4,3},{5,4},{6,5},{7,6},{8,7},{9,8},{10,9... | collective-permute-start | bytes 589832 | tf_op jit(solution)/shard_map/ppermute | solution.py:672
  24.7 0.0 collective-permute-start.2
  24.7 0.1 fusion.8.refs_3_
  24.9 0.0 collective-permute-done.1
  24.9 0.0 collective-permute-done
  24.9 4.0 %collective-permute-done.3.refs_2_ = bf16[8,96,128]{2,1,0:T(8,128)(2,1)S(1)} collective-permute-done((bf16[8,96,128]{2,1,0:T(8,128)(2,1)S(1)}, bf16[8,96,128]{2,1,0:T(8,128)(2,1)S(1)}, u32[]{:S(2)}, u32[]{:S(2)}) %collective-permute-start.3) | collective-permute-done | bytes 196640 | tf_op jit(solution)/shard_map/ppermute | solution.py:672
  28.9 6.3 %collective-permute-done.2.refs_0_ = bf16[8,96,128]{2,1,0:T(8,128)(2,1)S(1)} collective-permute-done((bf16[8,96,128]{2,1,0:T(8,128)(2,1)S(1)}, bf16[8,96,128]{2,1,0:T(8,128)(2,1)S(1)}, u32[]{:S(2)}, u32[]{:S(2)}) %collective-permute-start.2) | collective-permute-done | bytes 196640 | tf_op jit(solution)/shard_map/ppermute | solution.py:672
  35.2 20.3 %shard_map.129 = (bf16[8,216,128]{2,1,0:T(8,128)(2,1)}, f32[32,16,128]{2,1,0:T(8,128)S(1)}, bf16[6,74,48,384]{3,2,1,0:T(8,128)(2,1)}) custom-call(bf16[8,96,128]{2,1,0:T(8,128)(2,1)S(1)} %collective-permute-done.2.refs_0_, bf16[8,96,128]{2,1,0:T(8,128)(2,1)S(1)} %all-to-all-done.refs_1_, bf16[8,96,128]{2,1,0:T(8,128)(2,1)S(1)} %collective-permute-done.3.refs_2_, ...), custom_call_target="tpu_custom_call" | custom-call | flops 20000000000 | bytes 50000000 | tf_op jit(solution)/shard_map/pallas_call | solution.py:746
  55.6 0.0 copy-start.1
  55.6 0.0 copy-start.2
  55.6 19.5 %shard_map.131 = f32[32,24,128]{2,1,0:T(8,128)S(1)} custom-call(bf16[4,144,240]{2,1,0:T(8,128)(2,1)S(1)} %fusion.10.refs_0_, f32[32,16,128]{2,1,0:T(8,128)S(1)} %get-tuple-element.26.refs_1_, bf16[6,74,48,384]{3,2,1,0:T(8,128)(2,1)} %get-tuple-element.27.refs_2_), custom_call_target="tpu_custom_call" | custom-call | flops 20000000000 | bytes 50000000 | tf_op jit(solution)/shard_map/pallas_call | solution.py:765
  75.1 15.1 %all_to_all.20.recv_ref = f32[32,24,128]{2,1,0:T(8,128)S(1)} all-to-all(f32[32,24,128]{2,1,0:T(8,128)S(1)} %shard_map.131), channel_id=1, replica_groups=mesh['grp'=4,'slab'=8] {'grp','slab'}, dimensions={0} | all-to-all | bytes 786432 | tf_op jit(solution)/shard_map/all_to_all | solution.py:783
  90.3 3.5 %all-to-all-start.1 = ((bf16[8,216,128]{2,1,0:T(8,128)(2,1)}), bf16[8,216,128]{2,1,0:T(8,128)(2,1)S(1)}, u32[]{:S(2)}, u32[]{:S(2)}) async-start(bf16[8,216,128]{2,1,0:T(8,128)(2,1)} %get-tuple-element.25), calls=%async_computation.1 | async-start | bytes 884736 | tf_op jit(solution)/shard_map/all_to_all | solution.py:782
  93.7 0.8 constant_dynamic-update-slice_fusion.1
  94.5 0.6 constant_dynamic-update-slice_fusion
  95.2 4.7 %collective-permute-start.5 = (bf16[2016,128]{1,0:T(8,128)(2,1)}, bf16[2016,128]{1,0:T(8,128)(2,1)S(1)}, u32[]{:S(2)}, u32[]{:S(2)}) collective-permute-start(bf16[2016,128]{1,0:T(8,128)(2,1)} %constant_dynamic-update-slice_fusion), channel_id=1, source_target_pairs={{0,7},{1,0},{2,1},{3,2},{4,3},{5,4},{6,5},{7,6},{8,15},{9,8},{10,9... | collective-permute-start | bytes 1548296 | tf_op jit(solution)/shard_map/ppermute | solution.py:676
  99.8 0.0 collective-permute-start.4
  99.8 0.4 shard_map.132
  100.2 0.7 copy.30
  101.0 6.8 %all-to-all-done.1.st_ref = bf16[8,216,128]{2,1,0:T(8,128)(2,1)S(1)} async-done(((bf16[8,216,128]{2,1,0:T(8,128)(2,1)}), bf16[8,216,128]{2,1,0:T(8,128)(2,1)S(1)}, u32[]{:S(2)}, u32[]{:S(2)}) %all-to-all-start.1) | async-done | bytes 442400 | tf_op jit(solution)/shard_map/all_to_all | solution.py:782
  107.8 0.7 broadcast_in_dim.2
  108.5 12.5 %all-to-all-start.3 = ((f32[32,8,128]{2,1,0:T(8,128)}), f32[32,8,128]{2,1,0:T(8,128)S(1)}, u32[]{:S(2)}, u32[]{:S(2)}) async-start(f32[32,8,128]{2,1,0:T(8,128)} %broadcast_in_dim.2), calls=%async_computation.3 | async-start | bytes 262144 | tf_op jit(solution)/shard_map/all_to_all | solution.py:785
  121.0 2.7 %collective-permute-done.5.xr_ref = bf16[2016,128]{1,0:T(8,128)(2,1)S(1)} collective-permute-done((bf16[2016,128]{1,0:T(8,128)(2,1)}, bf16[2016,128]{1,0:T(8,128)(2,1)S(1)}, u32[]{:S(2)}, u32[]{:S(2)}) %collective-permute-start.5) | collective-permute-done | bytes 516128 | tf_op jit(solution)/shard_map/ppermute | solution.py:676
  123.7 0.0 collective-permute-done.4.xl_ref
  123.7 0.0 copy-done.1
  123.7 0.0 copy-done.2
  123.7 15.4 %shard_map.130 = f32[3,4,144,128]{3,2,1,0:T(8,128)} custom-call(f32[3,4,144,128]{3,2,1,0:T(8,128)S(1)} %copy-done.1, bf16[288,128]{1,0:T(8,128)(2,1)S(1)} %pad_maximum_fusion.1.ez_ref, bf16[2016,128]{1,0:T(8,128)(2,1)S(1)} %collective-permute-done.4.xl_ref, bf16[2016,128]{1,0:T(8,128)(2,1)S(1)} %collective-permute-done.5.xr_ref, ...), custom_call_target="tpu_custom_call" | custom-call | flops 15000000512 | bytes 37500000 | tf_op jit(solution)/shard_map/pallas_call | solution.py:788
  139.1 0.0 all-to-all-done.3
  139.1 0.3 shard_map.133
  139.4 0.8 copy.31
  140.2 0.7 copy.34
  140.9 0.8 copy.32
  141.8 0.8 copy.33
  (6 shorter events, 0.1 us)
Async XLA Ops:
  0.6 1.2 copy-start
  1.8 11.7 %copy-start.5 = (bf16[27,6,16]{0,2,1:T(8,128)(2,1)S(1)}, bf16[27,6,16]{0,2,1:T(8,128)(2,1)}, u32[]{:S(2)}) copy-start(bf16[27,6,16]{0,2,1:T(8,128)(2,1)} %param.12) | copy-start | bytes 15556
  1.8 11.8 %copy-start.6 = (bf16[27,16,3]{0,1,2:T(8,128)(2,1)S(1)}, bf16[27,16,3]{0,1,2:T(8,128)(2,1)}, u32[]{:S(2)}) copy-start(bf16[27,16,3]{0,1,2:T(8,128)(2,1)} %param.9) | copy-start | bytes 7780
  1.8 12.1 %copy-start.3 = (bf16[27,16,16]{0,2,1:T(8,128)(2,1)S(1)}, bf16[27,16,16]{0,2,1:T(8,128)(2,1)}, u32[]{:S(2)}) copy-start(bf16[27,16,16]{0,2,1:T(8,128)(2,1)} %param.10) | copy-start | bytes 41476
  1.8 12.3 %copy-start.4 = (bf16[27,16,16]{0,2,1:T(8,128)(2,1)S(1)}, bf16[27,16,16]{0,2,1:T(8,128)(2,1)}, u32[]{:S(2)}) copy-start(bf16[27,16,16]{0,2,1:T(8,128)(2,1)} %param.11) | copy-start | bytes 41476
  1.8 14.2 %copy-start.7 = (s32[4,1,256]{2,1,0:T(1,128)S(1)}, s32[4,1,256]{2,1,0:T(1,128)}, u32[]{:S(2)}) copy-start(s32[4,1,256]{2,1,0:T(1,128)} %constant.18.clone) | copy-start | bytes 12292
  1.8 14.2 %copy-start.8 = (s32[4,1,256]{2,1,0:T(1,128)S(1)}, s32[4,1,256]{2,1,0:T(1,128)}, u32[]{:S(2)}) copy-start(s32[4,1,256]{2,1,0:T(1,128)} %constant.17.clone) | copy-start | bytes 12292
  2.2 22.6 %collective-permute-start.1 = (bf16[144,128]{1,0:T(8,128)(2,1)S(1)}, bf16[144,128]{1,0:T(8,128)(2,1)S(1)}, u32[]{:S(2)}, u32[]{:S(2)}) collective-permute-start(bf16[144,128]{1,0:T(8,128)(2,1)S(1)} %get-tuple-element.19), channel_id=1, source_target_pairs={{0,24},{8,0},{16,8},{24,16},{1,25},{9,1},{17,9},{25,17},{2,26},{10... | collective-permute-start | bytes 110600 | tf_op jit(solution)/shard_map/ppermute | solution.py:676
  4.7 20.2 %collective-permute-start = (bf16[144,128]{1,0:T(8,128)(2,1)S(1)}, bf16[144,128]{1,0:T(8,128)(2,1)S(1)}, u32[]{:S(2)}, u32[]{:S(2)}) collective-permute-start(bf16[144,128]{1,0:T(8,128)(2,1)S(1)} %get-tuple-element.19), channel_id=1, source_target_pairs={{0,8},{8,16},{16,24},{24,0},{1,9},{9,17},{17,25},{25,1},{2,10},{10... | collective-permute-start | bytes 110600 | tf_op jit(solution)/shard_map/ppermute | solution.py:676
  7.7 14.7 %all-to-all-start = ((bf16[8,96,128]{2,1,0:T(8,128)(2,1)}), bf16[8,96,128]{2,1,0:T(8,128)(2,1)S(1)}, u32[]{:S(2)}, u32[]{:S(2)}) async-start(bf16[8,96,128]{2,1,0:T(8,128)(2,1)} %shard_map.128), calls=%async_computation | async-start | bytes 393216 | tf_op jit(solution)/shard_map/all_to_all | solution.py:710
  22.3 6.6 %collective-permute-start.3 = (bf16[8,96,128]{2,1,0:T(8,128)(2,1)S(1)}, bf16[8,96,128]{2,1,0:T(8,128)(2,1)S(1)}, u32[]{:S(2)}, u32[]{:S(2)}) collective-permute-start(bf16[8,96,128]{2,1,0:T(8,128)(2,1)S(1)} %all-to-all-done.refs_1_), channel_id=1, source_target_pairs={{0,31},{1,0},{2,1},{3,2},{4,3},{5,4},{6,5},{7,6},{8,7},{9,8},{10,9... | collective-permute-start | bytes 589832 | tf_op jit(solution)/shard_map/ppermute | solution.py:672
  24.7 10.5 %collective-permute-start.2 = (bf16[8,96,128]{2,1,0:T(8,128)(2,1)S(1)}, bf16[8,96,128]{2,1,0:T(8,128)(2,1)S(1)}, u32[]{:S(2)}, u32[]{:S(2)}) collective-permute-start(bf16[8,96,128]{2,1,0:T(8,128)(2,1)S(1)} %all-to-all-done.refs_1_), channel_id=1, source_target_pairs={{0,1},{1,2},{2,3},{3,4},{4,5},{5,6},{6,7},{7,8},{8,9},{9,10},{10,1... | collective-permute-start | bytes 589832 | tf_op jit(solution)/shard_map/ppermute | solution.py:672
  55.6 68.1 %copy-start.1 = (f32[3,4,144,128]{3,2,1,0:T(8,128)S(1)}, f32[3,4,144,128]{3,2,1,0:T(8,128)}, u32[]{:S(2)}) copy-start(f32[3,4,144,128]{3,2,1,0:T(8,128)} %v_ref.5) | copy-start | bytes 2654212
  55.6 68.1 %copy-start.2 = (s32[6,1,256]{2,1,0:T(1,128)S(1)}, s32[6,1,256]{2,1,0:T(1,128)}, u32[]{:S(2)}) copy-start(s32[6,1,256]{2,1,0:T(1,128)} %constant.19.clone.idx_ref) | copy-start | bytes 18436
  90.3 17.5 %all-to-all-start.1 = ((bf16[8,216,128]{2,1,0:T(8,128)(2,1)}), bf16[8,216,128]{2,1,0:T(8,128)(2,1)S(1)}, u32[]{:S(2)}, u32[]{:S(2)}) async-start(bf16[8,216,128]{2,1,0:T(8,128)(2,1)} %get-tuple-element.25), calls=%async_computation.1 | async-start | bytes 884736 | tf_op jit(solution)/shard_map/all_to_all | solution.py:782
  95.2 28.5 %collective-permute-start.5 = (bf16[2016,128]{1,0:T(8,128)(2,1)}, bf16[2016,128]{1,0:T(8,128)(2,1)S(1)}, u32[]{:S(2)}, u32[]{:S(2)}) collective-permute-start(bf16[2016,128]{1,0:T(8,128)(2,1)} %constant_dynamic-update-slice_fusion), channel_id=1, source_target_pairs={{0,7},{1,0},{2,1},{3,2},{4,3},{5,4},{6,5},{7,6},{8,15},{9,8},{10,9... | collective-permute-start | bytes 1548296 | tf_op jit(solution)/shard_map/ppermute | solution.py:676
  99.8 23.9 %collective-permute-start.4 = (bf16[2016,128]{1,0:T(8,128)(2,1)}, bf16[2016,128]{1,0:T(8,128)(2,1)S(1)}, u32[]{:S(2)}, u32[]{:S(2)}) collective-permute-start(bf16[2016,128]{1,0:T(8,128)(2,1)} %constant_dynamic-update-slice_fusion), channel_id=1, source_target_pairs={{0,1},{1,2},{2,3},{3,4},{4,5},{5,6},{6,7},{7,0},{8,9},{9,10},{10,1... | collective-permute-start | bytes 1548296 | tf_op jit(solution)/shard_map/ppermute | solution.py:676
  108.5 30.7 %all-to-all-start.3 = ((f32[32,8,128]{2,1,0:T(8,128)}), f32[32,8,128]{2,1,0:T(8,128)S(1)}, u32[]{:S(2)}, u32[]{:S(2)}) async-start(f32[32,8,128]{2,1,0:T(8,128)} %broadcast_in_dim.2), calls=%async_computation.3 | async-start | bytes 262144 | tf_op jit(solution)/shard_map/all_to_all | solution.py:785

commit v4 on v3

--- a/solution.py
+++ b/solution.py
@@ -19,7 +19,7 @@
 MARGIN = LAYERS + LAYERS - 1
 f32 = jnp.float32
 bf16 = jnp.bfloat16
-BATCH = 8
+BATCH = 24
 MIB = 1024 * 1024
 
 
@@ -162,24 +162,20 @@
         return value[:, t * lanes : (t + 1) * lanes]
 
     def after(value, t):
-        return jnp.where(
-            last_z, pltpu.roll(tile(value, t + 1), zl - 1, 1), pltpu.roll(tile(value, t), lanes - 1, 1)
-        )
+        mixed = jnp.where(first_z, tile(value, t + 1), tile(value, t))
+        return pltpu.roll(mixed, lanes - 1, 1)
 
     def before(value, t):
-        return jnp.where(
-            first_z,
-            pltpu.roll(tile(value, t - 1), lanes - (zl - 1), 1),
-            pltpu.roll(tile(value, t), 1, 1),
-        )
+        mixed = jnp.where(last_z, tile(value, t - 1), tile(value, t))
+        return pltpu.roll(mixed, 1, 1)
 
     def put(ref, y, value):
         for t in range(nt):
-            v = tile(value, t)
+            v = tile(value, t).astype(bf16)
             at = slice(t * lanes, (t + 1) * lanes)
-            ref[y + 1, 0:CH, at] = pltpu.roll(v, zl, 1).astype(bf16)
-            ref[y + 1, CH : 2 * CH, at] = v.astype(bf16)
-            ref[y + 1, 2 * CH : 3 * CH, at] = pltpu.roll(v, lanes - zl, 1).astype(bf16)
+            ref[y + 1, 0:CH, at] = pltpu.roll(v, zl, 1)
+            ref[y + 1, CH : 2 * CH, at] = v
+            ref[y + 1, 2 * CH : 3 * CH, at] = pltpu.roll(v, lanes - zl, 1)
 
     def put_cz(cz_ref, y, value):
         value = rounded(value)
@@ -252,8 +248,10 @@
         def swap(j, carry, t=t):
             base = pl.multiple_of(16 * j, 16)
             parts = granule_swap([tiles[t][s, pl.ds(base, 16), :].astype(f32) for s in range(n)])
+            turn = (t - hops) * zl % lanes
             for r in range(n):
-                f_ref[t, pl.ds(r * group + base, 16), :] = parts[r]
+                part = pltpu.roll(parts[r], turn, 1) if turn else parts[r]
+                f_ref[t, pl.ds(r * group + base, 16), :] = part
             return carry
 
         lax.fori_loop(0, group // 16, swap, 0)
@@ -631,7 +629,8 @@
                         x = (cx * d - 2 + xk) % total_x
                         z = z0 + e
                         t, zp = hops + z // zl, z % zl
-                        src = half * nt * lanes + t * lanes + x * zl + zp
+                        turned = (x + t - hops) % total_x
+                        src = half * nt * lanes + t * lanes + turned * zl + zp
                         lane = half * 64 + xk * window + e
                         table[variant, d // 2, 0, (d % 2) * 128 + lane] = src
     return table
@@ -725,8 +724,8 @@
 
     lower = [ring(mine, k) for k in range(hops, 0, -1)]
     upper = [ring(mine, -k) for k in range(1, hops + 1)]
-    edges, v16, lower, upper = lax.optimization_barrier((edges, v16, lower, upper))
     pack = jnp.concatenate([v16, edges], axis=0)
+    pack, lower, upper = lax.optimization_barrier((pack, lower, upper))
     pack_left = shift(pack, "slab", 1)
     pack_right = shift(pack, "slab", -1)
 
@@ -738,7 +737,7 @@
     per_device = round_up(-(-grad_rows // devices), 8)
     act = pltpu.VMEM((cy + 2, 3 * CH, nt * lanes), bf16)
     unroll = max(
-        u for u in range(1, cy + 1) if cy % u == 0 and u % (2 * SPAN) == 0 and u * nt <= 54
+        u for u in range(1, cy + 1) if cy % u == 0 and u % (2 * SPAN) == 0 and u * nt <= 108
     )
     dims = (n, hops, groups, devices, cy, cx, zl, length, unroll)
     act = ((cy + 2, 3 * CH, nt * lanes), bf16)

time: 143 us -> 132 us (0.923)
  Pallas kernels: 59.3 us -> 48.9 us
  waiting for transfers between devices: 26.1 us -> 21.1 us
  starting transfers between devices: 31.3 us -> 35.2 us
  blocking collectives: 15.1 us -> 17.2 us
    pallas_call x1, Pallas kernels: 19.5 us -> 12.9 us  [step(): call(functools.partial(backward_kernel, dims), jax.ShapeDtypeStruct((devi...]
    ppermute x2, waiting for transfers between devices: 10.3 us -> 5.04 us  [ring(): lax.ppermute(x, both, [(i, (i + shift) % devices) for i in range(devices)])]
    pallas_call x1, Pallas kernels: 20.3 us -> 16.6 us  [step(): call(functools.partial(forward_kernel, dims), (jax.ShapeDtypeStruct((n, 3...]
    ppermute x2, starting transfers between devices: 2.41 us -> 5.34 us  [ring(): lax.ppermute(x, both, [(i, (i + shift) % devices) for i in range(devices)])]
    all_to_all x1, blocking collectives: 15.1 us -> 17.2 us  [step(): arrived = lax.all_to_all(to_sum, both, 0, 0, tiled=True)]
    unnamed x28 -> x27, local copies, waits for them, and re-layouts: 6.69 us -> 5.9 us
  transfers between devices with their start and end apart: 9 -> 9, of which waited for: 5 -> 6; matrix products, arithmetic and copies ran while one was open for 4% -> 3% of each run, Pallas kernels for 13% -> 14%
where the time goes in v4:
time: 132 us
  Pallas kernels  48.9 us (37%)
  starting transfers between devices  35.2 us (27%)
  waiting for transfers between devices  21.1 us (16%)
  blocking collectives  17.2 us (13%)
  local copies, waits for them, and re-layouts  7.99 us (6%)
    all_to_all x1, blocking collectives, step(): arrived = lax.all_to_all(to_sum, both, 0, 0, tiled=True)  17.2 us
    pallas_call x1, Pallas kernels, step(): call(functools.partial(forward_kernel, dims), (jax.ShapeDtypeStruct((n, 3...  16.6 us
    pallas_call x1, Pallas kernels, step(): call(functools.partial(advance_kernel, n), jax.ShapeDtypeStruct(velocity....  15.4 us
    pallas_call x1, Pallas kernels, step(): call(functools.partial(backward_kernel, dims), jax.ShapeDtypeStruct((devi...  12.9 us
    all_to_all x1, starting transfers between devices, step(): lax.all_to_all(jnp.broadcast_to(total[None], (devices, per_device, 128)),...  12.5 us
    all_to_all x1, waiting for transfers between devices, step(): st = lax.all_to_all(bsend, 'slab', 0, 0, tiled=True)  8.1 us
    ppermute x4, starting transfers between devices, shift(): return lax.ppermute(x, axis, [(i, (i + by) % count) for i in range(count)])  7.33 us
    all_to_all x1, starting transfers between devices, step(): mine = lax.all_to_all(fields, 'slab', 0, 0, tiled=True)  6.53 us
  transfers between devices with their start and end apart: 9, of which 6 were waited for; matrix products, arithmetic and copies ran while one was open for 3% of the time, Pallas kernels for 14%

profile of v4, /device:TPU:0, one launch (start us, length us, event | category | flops | bytes accessed | tf_op | source)
XLA Modules:
  0.0 131.8 jit_solution(8941649894273422828)
XLA Ops:
  0.6 0.0 copy-start
  0.6 1.2 copy-done
  1.8 0.0 copy-start.6
  1.8 0.0 copy-start.5
  1.8 0.0 copy-start.3
  1.8 0.0 copy-start.4
  1.8 0.0 copy-start.7
  1.8 0.0 copy-start.8
  1.8 0.4 shard_map.127
  2.2 0.5 collective-permute-start
  2.8 2.0 %collective-permute-start.1 = (bf16[144,128]{1,0:T(8,128)(2,1)S(1)}, bf16[144,128]{1,0:T(8,128)(2,1)S(1)}, u32[]{:S(2)}, u32[]{:S(2)}) collective-permute-start(bf16[144,128]{1,0:T(8,128)(2,1)S(1)} %get-tuple-element.18), channel_id=1, source_target_pairs={{0,24},{8,0},{16,8},{24,16},{1,25},{9,1},{17,9},{25,17},{2,26},{10... | collective-permute-start | bytes 110600 | tf_op jit(solution)/shard_map/ppermute | solution.py:675
  4.8 2.9 %shard_map.128 = bf16[8,96,128]{2,1,0:T(8,128)(2,1)} custom-call(f32[3,4,144,128]{3,2,1,0:T(8,128)S(1)} %copy-done), custom_call_target="tpu_custom_call" | custom-call | flops 4000000000 | bytes 10000000 | tf_op jit(solution)/shard_map/pallas_call | solution.py:702
  7.7 6.5 %all-to-all-start = ((bf16[8,96,128]{2,1,0:T(8,128)(2,1)}), bf16[8,96,128]{2,1,0:T(8,128)(2,1)S(1)}, u32[]{:S(2)}, u32[]{:S(2)}) async-start(bf16[8,96,128]{2,1,0:T(8,128)(2,1)} %shard_map.128), calls=%async_computation | async-start | bytes 393216 | tf_op jit(solution)/shard_map/all_to_all | solution.py:709
  14.3 0.0 copy-done.6
  14.3 0.2 copy.24
  14.5 0.0 copy-done.5
  14.5 0.1 copy.27
  14.7 0.0 copy-done.3
  14.7 0.2 copy.25
  14.9 0.0 copy-done.4
  14.9 0.2 copy.26
  15.1 0.1 pad_maximum_fusion.1
  15.3 0.3 copy.28
  15.5 0.3 reshape.31
  15.8 0.1 fusion.8.refs_3_
  16.0 0.5 copy.29
  16.5 0.3 reshape.32
  16.8 0.0 copy-done.7
  16.8 0.0 copy-done.8
  16.8 0.1 fusion.10.refs_0_
  17.0 5.3 %all-to-all-done.refs_1_ = bf16[8,96,128]{2,1,0:T(8,128)(2,1)S(1)} async-done(((bf16[8,96,128]{2,1,0:T(8,128)(2,1)}), bf16[8,96,128]{2,1,0:T(8,128)(2,1)S(1)}, u32[]{:S(2)}, u32[]{:S(2)}) %all-to-all-start) | async-done | bytes 196640 | tf_op jit(solution)/shard_map/all_to_all | solution.py:709
  22.3 1.0 collective-permute-start.2
  23.3 4.3 %collective-permute-start.3 = (bf16[8,96,128]{2,1,0:T(8,128)(2,1)S(1)}, bf16[8,96,128]{2,1,0:T(8,128)(2,1)S(1)}, u32[]{:S(2)}, u32[]{:S(2)}) collective-permute-start(bf16[8,96,128]{2,1,0:T(8,128)(2,1)S(1)} %all-to-all-done.refs_1_), channel_id=1, source_target_pairs={{0,31},{1,0},{2,1},{3,2},{4,3},{5,4},{6,5},{7,6},{8,7},{9,8},{10,9... | collective-permute-start | bytes 589832 | tf_op jit(solution)/shard_map/ppermute | solution.py:671
  27.6 0.0 collective-permute-done
  27.6 0.0 collective-permute-done.1
  27.7 3.3 %collective-permute-done.2.refs_0_ = bf16[8,96,128]{2,1,0:T(8,128)(2,1)S(1)} collective-permute-done((bf16[8,96,128]{2,1,0:T(8,128)(2,1)S(1)}, bf16[8,96,128]{2,1,0:T(8,128)(2,1)S(1)}, u32[]{:S(2)}, u32[]{:S(2)}) %collective-permute-start.2) | collective-permute-done | bytes 196640 | tf_op jit(solution)/shard_map/ppermute | solution.py:671
  31.0 1.7 %collective-permute-done.3.refs_2_ = bf16[8,96,128]{2,1,0:T(8,128)(2,1)S(1)} collective-permute-done((bf16[8,96,128]{2,1,0:T(8,128)(2,1)S(1)}, bf16[8,96,128]{2,1,0:T(8,128)(2,1)S(1)}, u32[]{:S(2)}, u32[]{:S(2)}) %collective-permute-start.3) | collective-permute-done | bytes 196640 | tf_op jit(solution)/shard_map/ppermute | solution.py:671
  32.7 16.6 %shard_map.129 = (bf16[8,216,128]{2,1,0:T(8,128)(2,1)}, f32[32,16,128]{2,1,0:T(8,128)S(1)}, bf16[6,74,48,384]{3,2,1,0:T(8,128)(2,1)}) custom-call(bf16[8,96,128]{2,1,0:T(8,128)(2,1)S(1)} %collective-permute-done.2.refs_0_, bf16[8,96,128]{2,1,0:T(8,128)(2,1)S(1)} %all-to-all-done.refs_1_, bf16[8,96,128]{2,1,0:T(8,128)(2,1)S(1)} %collective-permute-done.3.refs_2_, ...), custom_call_target="tpu_custom_call" | custom-call | flops 20000000000 | bytes 50000000 | tf_op jit(solution)/shard_map/pallas_call | solution.py:745
  49.3 0.0 copy-start.1
  49.3 0.0 copy-start.2
  49.3 12.9 %shard_map.131 = f32[32,24,128]{2,1,0:T(8,128)S(1)} custom-call(bf16[4,144,240]{2,1,0:T(8,128)(2,1)S(1)} %fusion.10.refs_0_, f32[32,16,128]{2,1,0:T(8,128)S(1)} %get-tuple-element.24.refs_1_, bf16[6,74,48,384]{3,2,1,0:T(8,128)(2,1)} %get-tuple-element.25.refs_2_), custom_call_target="tpu_custom_call" | custom-call | flops 20000000000 | bytes 50000000 | tf_op jit(solution)/shard_map/pallas_call | solution.py:764
  62.2 17.2 %all_to_all.20.recv_ref = f32[32,24,128]{2,1,0:T(8,128)S(1)} all-to-all(f32[32,24,128]{2,1,0:T(8,128)S(1)} %shard_map.131), channel_id=1, replica_groups=mesh['grp'=4,'slab'=8] {'grp','slab'}, dimensions={0} | all-to-all | bytes 786432 | tf_op jit(solution)/shard_map/all_to_all | solution.py:782
  79.4 3.5 %all-to-all-start.1 = ((bf16[8,216,128]{2,1,0:T(8,128)(2,1)}), bf16[8,216,128]{2,1,0:T(8,128)(2,1)S(1)}, u32[]{:S(2)}, u32[]{:S(2)}) async-start(bf16[8,216,128]{2,1,0:T(8,128)(2,1)} %get-tuple-element.23), calls=%async_computation.1 | async-start | bytes 884736 | tf_op jit(solution)/shard_map/all_to_all | solution.py:781
  82.9 1.9 %collective-permute-start.4 = (bf16[2016,128]{1,0:T(8,128)(2,1)S(1)}, bf16[2016,128]{1,0:T(8,128)(2,1)S(1)}, u32[]{:S(2)}, u32[]{:S(2)}) collective-permute-start(bf16[2016,128]{1,0:T(8,128)(2,1)S(1)} %pad_maximum_fusion), channel_id=1, source_target_pairs={{0,1},{1,2},{2,3},{3,4},{4,5},{5,6},{6,7},{7,0},{8,9},{9,10},{10,1... | collective-permute-start | bytes 1548296 | tf_op jit(solution)/shard_map/ppermute | solution.py:675
  84.8 2.9 %collective-permute-start.5 = (bf16[2016,128]{1,0:T(8,128)(2,1)S(1)}, bf16[2016,128]{1,0:T(8,128)(2,1)S(1)}, u32[]{:S(2)}, u32[]{:S(2)}) collective-permute-start(bf16[2016,128]{1,0:T(8,128)(2,1)S(1)} %pad_maximum_fusion), channel_id=1, source_target_pairs={{0,7},{1,0},{2,1},{3,2},{4,3},{5,4},{6,5},{7,6},{8,15},{9,8},{10,9... | collective-permute-start | bytes 1548296 | tf_op jit(solution)/shard_map/ppermute | solution.py:675
  87.7 0.4 shard_map.132
  88.1 0.7 copy.30
  88.9 8.1 %all-to-all-done.1.st_ref = bf16[8,216,128]{2,1,0:T(8,128)(2,1)S(1)} async-done(((bf16[8,216,128]{2,1,0:T(8,128)(2,1)}), bf16[8,216,128]{2,1,0:T(8,128)(2,1)S(1)}, u32[]{:S(2)}, u32[]{:S(2)}) %all-to-all-start.1) | async-done | bytes 442400 | tf_op jit(solution)/shard_map/all_to_all | solution.py:781
  97.0 0.7 broadcast_in_dim.2
  97.6 12.5 %all-to-all-start.3 = ((f32[32,8,128]{2,1,0:T(8,128)}), f32[32,8,128]{2,1,0:T(8,128)S(1)}, u32[]{:S(2)}, u32[]{:S(2)}) async-start(f32[32,8,128]{2,1,0:T(8,128)} %broadcast_in_dim.2), calls=%async_computation.3 | async-start | bytes 262144 | tf_op jit(solution)/shard_map/all_to_all | solution.py:784
  110.2 0.3 collective-permute-done.4.xl_ref
  110.4 2.4 %collective-permute-done.5.xr_ref = bf16[2016,128]{1,0:T(8,128)(2,1)S(1)} collective-permute-done((bf16[2016,128]{1,0:T(8,128)(2,1)S(1)}, bf16[2016,128]{1,0:T(8,128)(2,1)S(1)}, u32[]{:S(2)}, u32[]{:S(2)}) %collective-permute-start.5) | collective-permute-done | bytes 516128 | tf_op jit(solution)/shard_map/ppermute | solution.py:675
  112.9 0.0 copy-done.1
  112.9 0.0 copy-done.2
  112.9 15.4 %shard_map.130 = f32[3,4,144,128]{3,2,1,0:T(8,128)} custom-call(f32[3,4,144,128]{3,2,1,0:T(8,128)S(1)} %copy-done.1, bf16[288,128]{1,0:T(8,128)(2,1)S(1)} %pad_maximum_fusion.2.ez_ref, bf16[2016,128]{1,0:T(8,128)(2,1)S(1)} %collective-permute-done.4.xl_ref, bf16[2016,128]{1,0:T(8,128)(2,1)S(1)} %collective-permute-done.5.xr_ref, ...), custom_call_target="tpu_custom_call" | custom-call | flops 15000000512 | bytes 37500000 | tf_op jit(solution)/shard_map/pallas_call | solution.py:787
  128.3 0.0 all-to-all-done.3
  128.3 0.3 shard_map.133
  128.5 0.8 copy.32
  129.4 0.8 copy.33
  130.2 0.7 copy.34
  130.9 0.8 copy.31
  (7 shorter events, 0.2 us)
Async XLA Ops:
  0.6 1.2 copy-start
  1.8 12.5 %copy-start.6 = (bf16[27,16,3]{0,1,2:T(8,128)(2,1)S(1)}, bf16[27,16,3]{0,1,2:T(8,128)(2,1)}, u32[]{:S(2)}) copy-start(bf16[27,16,3]{0,1,2:T(8,128)(2,1)} %param.9) | copy-start | bytes 7780
  1.8 12.7 %copy-start.5 = (bf16[27,6,16]{0,2,1:T(8,128)(2,1)S(1)}, bf16[27,6,16]{0,2,1:T(8,128)(2,1)}, u32[]{:S(2)}) copy-start(bf16[27,6,16]{0,2,1:T(8,128)(2,1)} %param.12) | copy-start | bytes 15556
  1.8 12.9 %copy-start.3 = (bf16[27,16,16]{0,2,1:T(8,128)(2,1)S(1)}, bf16[27,16,16]{0,2,1:T(8,128)(2,1)}, u32[]{:S(2)}) copy-start(bf16[27,16,16]{0,2,1:T(8,128)(2,1)} %param.10) | copy-start | bytes 41476
  1.8 13.1 %copy-start.4 = (bf16[27,16,16]{0,2,1:T(8,128)(2,1)S(1)}, bf16[27,16,16]{0,2,1:T(8,128)(2,1)}, u32[]{:S(2)}) copy-start(bf16[27,16,16]{0,2,1:T(8,128)(2,1)} %param.11) | copy-start | bytes 41476
  1.8 15.0 %copy-start.7 = (s32[4,1,256]{2,1,0:T(1,128)S(1)}, s32[4,1,256]{2,1,0:T(1,128)}, u32[]{:S(2)}) copy-start(s32[4,1,256]{2,1,0:T(1,128)} %constant.17.clone) | copy-start | bytes 12292
  1.8 15.0 %copy-start.8 = (s32[4,1,256]{2,1,0:T(1,128)S(1)}, s32[4,1,256]{2,1,0:T(1,128)}, u32[]{:S(2)}) copy-start(s32[4,1,256]{2,1,0:T(1,128)} %constant.18.clone) | copy-start | bytes 12292
  2.2 25.4 %collective-permute-start = (bf16[144,128]{1,0:T(8,128)(2,1)S(1)}, bf16[144,128]{1,0:T(8,128)(2,1)S(1)}, u32[]{:S(2)}, u32[]{:S(2)}) collective-permute-start(bf16[144,128]{1,0:T(8,128)(2,1)S(1)} %get-tuple-element.18), channel_id=1, source_target_pairs={{0,8},{8,16},{16,24},{24,0},{1,9},{9,17},{17,25},{25,1},{2,10},{10... | collective-permute-start | bytes 110600 | tf_op jit(solution)/shard_map/ppermute | solution.py:675
  2.8 24.8 %collective-permute-start.1 = (bf16[144,128]{1,0:T(8,128)(2,1)S(1)}, bf16[144,128]{1,0:T(8,128)(2,1)S(1)}, u32[]{:S(2)}, u32[]{:S(2)}) collective-permute-start(bf16[144,128]{1,0:T(8,128)(2,1)S(1)} %get-tuple-element.18), channel_id=1, source_target_pairs={{0,24},{8,0},{16,8},{24,16},{1,25},{9,1},{17,9},{25,17},{2,26},{10... | collective-permute-start | bytes 110600 | tf_op jit(solution)/shard_map/ppermute | solution.py:675
  7.7 14.5 %all-to-all-start = ((bf16[8,96,128]{2,1,0:T(8,128)(2,1)}), bf16[8,96,128]{2,1,0:T(8,128)(2,1)S(1)}, u32[]{:S(2)}, u32[]{:S(2)}) async-start(bf16[8,96,128]{2,1,0:T(8,128)(2,1)} %shard_map.128), calls=%async_computation | async-start | bytes 393216 | tf_op jit(solution)/shard_map/all_to_all | solution.py:709
  22.3 8.7 %collective-permute-start.2 = (bf16[8,96,128]{2,1,0:T(8,128)(2,1)S(1)}, bf16[8,96,128]{2,1,0:T(8,128)(2,1)S(1)}, u32[]{:S(2)}, u32[]{:S(2)}) collective-permute-start(bf16[8,96,128]{2,1,0:T(8,128)(2,1)S(1)} %all-to-all-done.refs_1_), channel_id=1, source_target_pairs={{0,1},{1,2},{2,3},{3,4},{4,5},{5,6},{6,7},{7,8},{8,9},{9,10},{10,1... | collective-permute-start | bytes 589832 | tf_op jit(solution)/shard_map/ppermute | solution.py:671
  23.3 9.4 %collective-permute-start.3 = (bf16[8,96,128]{2,1,0:T(8,128)(2,1)S(1)}, bf16[8,96,128]{2,1,0:T(8,128)(2,1)S(1)}, u32[]{:S(2)}, u32[]{:S(2)}) collective-permute-start(bf16[8,96,128]{2,1,0:T(8,128)(2,1)S(1)} %all-to-all-done.refs_1_), channel_id=1, source_target_pairs={{0,31},{1,0},{2,1},{3,2},{4,3},{5,4},{6,5},{7,6},{8,7},{9,8},{10,9... | collective-permute-start | bytes 589832 | tf_op jit(solution)/shard_map/ppermute | solution.py:671
  49.3 63.6 %copy-start.1 = (f32[3,4,144,128]{3,2,1,0:T(8,128)S(1)}, f32[3,4,144,128]{3,2,1,0:T(8,128)}, u32[]{:S(2)}) copy-start(f32[3,4,144,128]{3,2,1,0:T(8,128)} %v_ref.5) | copy-start | bytes 2654212
  49.3 63.6 %copy-start.2 = (s32[6,1,256]{2,1,0:T(1,128)S(1)}, s32[6,1,256]{2,1,0:T(1,128)}, u32[]{:S(2)}) copy-start(s32[6,1,256]{2,1,0:T(1,128)} %constant.19.clone.idx_ref) | copy-start | bytes 18436
  79.4 17.5 %all-to-all-start.1 = ((bf16[8,216,128]{2,1,0:T(8,128)(2,1)}), bf16[8,216,128]{2,1,0:T(8,128)(2,1)S(1)}, u32[]{:S(2)}, u32[]{:S(2)}) async-start(bf16[8,216,128]{2,1,0:T(8,128)(2,1)} %get-tuple-element.23), calls=%async_computation.1 | async-start | bytes 884736 | tf_op jit(solution)/shard_map/all_to_all | solution.py:781
  82.9 27.5 %collective-permute-start.4 = (bf16[2016,128]{1,0:T(8,128)(2,1)S(1)}, bf16[2016,128]{1,0:T(8,128)(2,1)S(1)}, u32[]{:S(2)}, u32[]{:S(2)}) collective-permute-start(bf16[2016,128]{1,0:T(8,128)(2,1)S(1)} %pad_maximum_fusion), channel_id=1, source_target_pairs={{0,1},{1,2},{2,3},{3,4},{4,5},{5,6},{6,7},{7,0},{8,9},{9,10},{10,1... | collective-permute-start | bytes 1548296 | tf_op jit(solution)/shard_map/ppermute | solution.py:675
  84.8 28.1 %collective-permute-start.5 = (bf16[2016,128]{1,0:T(8,128)(2,1)S(1)}, bf16[2016,128]{1,0:T(8,128)(2,1)S(1)}, u32[]{:S(2)}, u32[]{:S(2)}) collective-permute-start(bf16[2016,128]{1,0:T(8,128)(2,1)S(1)} %pad_maximum_fusion), channel_id=1, source_target_pairs={{0,7},{1,0},{2,1},{3,2},{4,3},{5,4},{6,5},{7,6},{8,15},{9,8},{10,9... | collective-permute-start | bytes 1548296 | tf_op jit(solution)/shard_map/ppermute | solution.py:675
  97.6 30.7 %all-to-all-start.3 = ((f32[32,8,128]{2,1,0:T(8,128)}), f32[32,8,128]{2,1,0:T(8,128)S(1)}, u32[]{:S(2)}, u32[]{:S(2)}) async-start(f32[32,8,128]{2,1,0:T(8,128)} %broadcast_in_dim.2), calls=%async_computation.3 | async-start | bytes 262144 | tf_op jit(solution)/shard_map/all_to_all | solution.py:784
